TPU v7x, 32 devices: a whole 2x2x4 slice. The times are simulated.
32 devices in a mesh: dp: 8 (over y, x, core), hid: 4 (over z).
Axes of the slice: x: 2, y: 2, z: 4, core: 2. Of those that a mesh axis runs over, the one named last changes fastest.
Arguments:
- tokens: bfloat16 [8, 1024, 768], P('dp', 'hid'), may hold values from -6 to 6
- cotangent: bfloat16 [8, 1024, 768], P('dp', 'hid'), may hold values from -6 to 6
- item_lengths: int32 [8], P('dp'), may hold values from 256 to 1024, as said below
- time_steps: int32 [8], P('dp'), may hold values from 0 to 999
- class_labels: int32 [8], P('dp'), may hold values from 0 to 999
- routes: int32 [8, 1024, 2], P('dp'), may hold values from 0 to 7, all different within a row; in each aligned block of 1024 rows (0 to 1023, 1024 to 2047, ..., all dimensions but the last counted through in order) at most 320 rows name the same one
- time_table: bfloat16 [1000, 768], P('hid'), may hold values from -6 to 6
- class_table: bfloat16 [1000, 768], P('hid'), may hold values from -6 to 6
- modulation: bfloat16 [768, 4608], P('hid'), may hold values from -0.21875 to 0.21875
- qkv_weight: bfloat16 [768, 2304], P('hid'), may hold values from -0.21875 to 0.21875
- out_weight: bfloat16 [768, 768], P('hid'), may hold values from -1.5 to 1.5
- router: bfloat16 [768, 8], P('hid'), may hold values from -0.119628906 to 0.119628906
- shared_up: bfloat16 [768, 3072], P(None, 'hid'), may hold values from -0.21875 to 0.21875
- shared_down: bfloat16 [3072, 768], P('hid'), may hold values from -0.109375 to 0.109375
- expert_up: bfloat16 [8, 768, 3072], P('dp', None, 'hid'), may hold values from -0.21875 to 0.21875
- expert_down: bfloat16 [8, 3072, 768], P('dp', 'hid'), may hold values from -0.109375 to 0.109375
Outputs:
- output: bfloat16 [8, 1024, 768], P('dp', 'hid')
- tokens_grad: float32 [8, 1024, 768], P('dp', 'hid')
- time_table_grad: float32 [1000, 768], P('hid')
- class_table_grad: float32 [1000, 768], P('hid')
- modulation_grad: float32 [768, 4608], P('hid')
- qkv_weight_grad: float32 [768, 2304], P('hid')
- out_weight_grad: float32 [768, 768], P('hid')
- router_grad: float32 [768, 8], P('hid')
- shared_up_grad: float32 [768, 3072], P(None, 'hid')
- shared_down_grad: float32 [3072, 768], P('hid')
- expert_up_grad: float32 [8, 768, 3072], P('dp', None, 'hid')
- expert_down_grad: float32 [8, 3072, 768], P('dp', 'hid')
Inputs may be any that keep to these rules, and one draw needn't show every extreme that they name: `routes`: the 2 experts of a patch differ. Among the patches of the 1 items of one index of dp, no expert is named by more than 320 patches, and in some index of dp some expert is named by exactly 320. `item_lengths`: each item has 256 or 1024 valid patches at its front; the rest are padding, which is never a key.
All inputs are finite; a program needn't handle non-finite values.
Results may differ from a plain program's by a relative error of at most 0.023.
Values may be sent and summed in bfloat16 or wider, within the bound.
No kernel may reach another device: no remote copies, remote signals or barrier semaphores. Data moves between devices by JAX's collectives and lax.ppermute only.
A program may use at most 256 MiB of HBM per device.

v0:
```python
import jax
import jax.numpy as jnp
from jax import lax
from jax.sharding import PartitionSpec as P

HEADS = 12
HDIM = 64


def layer_norm(values):
    center = values - jnp.mean(values, axis=-1, keepdims=True)
    inverse = lax.rsqrt(jnp.mean(center * center, axis=-1, keepdims=True) + 1e-06)
    return (center * inverse, inverse)


def norm_back(grad_norm, normed, inverse):
    first = jnp.mean(grad_norm, axis=-1, keepdims=True)
    second = jnp.mean(grad_norm * normed, axis=-1, keepdims=True)
    return inverse * (grad_norm - first - normed * second)


def gelu_tanh(values):
    return (
        0.5
        * values
        * (1.0 + jnp.tanh(0.7978845608028654 * (values + 0.044715 * values * values * values)))
    )


def gelu_back(pre_act, grad_act):
    return jax.vjp(gelu_tanh, pre_act)[1](grad_act)[0]


def silu_back(cond, grad_out):
    return jax.vjp(jax.nn.silu, cond)[1](grad_out)[0]


def exact_dot(left, right):
    return jnp.dot(left, right, precision=lax.Precision.HIGHEST, preferred_element_type=jnp.float32)


def shards(
    tokens,
    cotangent,
    item_lengths,
    time_steps,
    class_labels,
    routes,
    time_table,
    class_table,
    modulation,
    qkv_weight,
    out_weight,
    router,
    shared_up,
    shared_down,
    expert_up,
    expert_down,
):
    hid_count = lax.axis_size("hid")
    dp_count = lax.axis_size("dp")
    hid_rank = lax.axis_index("hid")
    item_count, local_len, model_width = tokens.shape
    full_len = routes.shape[1]
    top_count = routes.shape[2]
    capacity = item_count * full_len * top_count * 5 // (4 * dp_count)
    gathered = (
        lax.all_gather(qkv_weight, "hid", axis=0, tiled=True),
        lax.all_gather(out_weight, "hid", axis=0, tiled=True),
        lax.all_gather(router, "hid", axis=0, tiled=True),
        lax.all_gather(modulation, "hid", axis=0, tiled=True),
        lax.all_gather(time_table, "hid", axis=0, tiled=True),
        lax.all_gather(class_table, "hid", axis=0, tiled=True),
    )
    qkv_full, out_full, router_full, modulation_full, time_full, class_full = gathered
    time_hot = (
        time_steps[:, None] == jnp.arange(time_full.shape[0], dtype=jnp.int32)[None, :]
    ).astype(jnp.bfloat16)
    class_hot = (
        class_labels[:, None] == jnp.arange(class_full.shape[0], dtype=jnp.int32)[None, :]
    ).astype(jnp.bfloat16)
    cond = jnp.dot(time_hot, time_full, preferred_element_type=jnp.float32) + jnp.dot(
        class_hot, class_full, preferred_element_type=jnp.float32
    )
    scaled = jax.nn.silu(cond).astype(jnp.bfloat16)
    shifts = jnp.dot(scaled, modulation_full, preferred_element_type=jnp.float32).reshape(
        item_count, 6, 1, model_width
    )
    shift_in = shifts[:, 0]
    scale_in = shifts[:, 1]
    gate_in = shifts[:, 2]
    shift_mid = shifts[:, 3]
    scale_mid = shifts[:, 4]
    gate_mid = shifts[:, 5]
    tokens_f = tokens.astype(jnp.float32)
    normed_in, inverse_in = layer_norm(tokens_f)
    hidden_in = (normed_in * (1.0 + scale_in) + shift_in).astype(jnp.bfloat16)
    row_count = item_count * local_len
    in_rows = hidden_in.reshape(row_count, model_width)
    projected = jnp.dot(in_rows, qkv_full, preferred_element_type=jnp.float32).astype(jnp.bfloat16)
    projected = projected.reshape(item_count, local_len, 3 * model_width)
    queries = projected[:, :, :model_width].reshape(item_count, local_len, HEADS, HDIM)
    key_values = lax.all_gather(projected[None, :, :, model_width:], "hid", axis=0, tiled=True)
    key_rows = key_values[..., :model_width].reshape(hid_count, item_count, local_len, HEADS, HDIM)
    value_rows = key_values[..., model_width:].reshape(
        hid_count, item_count, local_len, HEADS, HDIM
    )
    head_scale = HDIM ** (-0.5)
    positions = jnp.arange(hid_count * local_len, dtype=jnp.int32).reshape(hid_count, local_len)
    valid_keys = (positions[None] < item_lengths[:, None, None])[:, None, None]

    def masked_scores():
        raw_scores = (
            jnp.einsum("iqhd,kilhd->ihqkl", queries, key_rows, preferred_element_type=jnp.float32)
            * head_scale
        )
        return jnp.where(valid_keys, raw_scores, -1e30)

    scores = masked_scores()
    top_score = jnp.max(scores, axis=(3, 4), keepdims=True)
    log_total = top_score + jnp.log(
        jnp.sum(jnp.exp(scores - top_score), axis=(3, 4), keepdims=True)
    )
    soft_low = jnp.exp(scores - log_total).astype(jnp.bfloat16)
    attended = jnp.einsum(
        "ihqkl,kilhd->iqhd", soft_low, value_rows, preferred_element_type=jnp.float32
    )
    attended = attended.astype(jnp.bfloat16).reshape(row_count, model_width)
    branch = jnp.dot(attended, out_full, preferred_element_type=jnp.float32).reshape(
        item_count, local_len, model_width
    )
    residual = tokens_f + gate_in * branch
    normed_mid, inverse_mid = layer_norm(residual)
    hidden_mid = (normed_mid * (1.0 + scale_mid) + shift_mid).astype(jnp.bfloat16)
    mid_own_rows = hidden_mid.reshape(row_count, model_width)
    logits = jnp.dot(mid_own_rows, router_full, preferred_element_type=jnp.float32).reshape(
        item_count, local_len, 1, dp_count
    )
    own_routes = lax.dynamic_slice_in_dim(routes, hid_rank * local_len, local_len, 1)
    route_hot = (own_routes[..., None] == jnp.arange(dp_count, dtype=jnp.int32)).astype(jnp.float32)
    picked = jnp.sum(route_hot * logits, axis=-1)
    top_pick = jnp.max(picked, axis=-1, keepdims=True)
    exp_terms = jnp.exp(picked - top_pick)
    gate_soft = exp_terms / jnp.sum(exp_terms, axis=-1, keepdims=True)
    gates_low = gate_soft.astype(jnp.bfloat16)
    mid_all, gate_all = (
        lax.all_gather(hidden_mid[None], "hid", axis=0, tiled=True),
        lax.all_gather(gates_low[None], "hid", axis=0, tiled=True),
    )
    group_rows = hid_count * row_count
    mid_rows = mid_all.reshape(group_rows, model_width)
    shared_pre = jnp.dot(mid_rows, shared_up, preferred_element_type=jnp.float32)
    shared_act = gelu_tanh(shared_pre).astype(jnp.bfloat16)
    shared_out = jnp.dot(shared_act, shared_down, preferred_element_type=jnp.float32)
    group_routes = (
        routes.reshape(item_count, hid_count, local_len, top_count)
        .transpose(1, 0, 2, 3)
        .reshape(-1)
    )
    expert_hot = (group_routes[:, None] == jnp.arange(dp_count, dtype=jnp.int32)[None, :]).astype(
        jnp.int32
    )
    slot_of = jnp.sum(jnp.cumsum(expert_hot, axis=0) * expert_hot, axis=1) - 1
    target = group_routes * capacity + slot_of
    pair_count = group_rows * top_count
    pair_of = (
        jnp.full((dp_count * capacity,), pair_count, jnp.int32)
        .at[target]
        .set(jnp.arange(pair_count, dtype=jnp.int32))
    )
    token_of = pair_of // top_count
    rows_pad = jnp.concatenate([mid_rows, jnp.zeros((1, model_width), jnp.bfloat16)], axis=0)
    gates_pad = jnp.concatenate([gate_all.reshape(-1), jnp.zeros((1,), jnp.bfloat16)])
    send_rows = jnp.take(rows_pad, token_of, axis=0).reshape(dp_count, capacity, model_width)
    send_gates = jnp.take(gates_pad, pair_of).reshape(dp_count, capacity)
    expert_in, expert_gates = (
        lax.all_to_all(send_rows, "dp", split_axis=0, concat_axis=0, tiled=True),
        lax.all_to_all(send_gates, "dp", split_axis=0, concat_axis=0, tiled=True),
    )
    slot_rows = dp_count * capacity
    expert_rows = expert_in.reshape(slot_rows, model_width)
    gate_col = expert_gates.reshape(slot_rows, 1).astype(jnp.float32)
    expert_pre = jnp.dot(expert_rows, expert_up[0], preferred_element_type=jnp.float32)
    expert_gelu = gelu_tanh(expert_pre)
    expert_act = (gate_col * expert_gelu).astype(jnp.bfloat16)
    expert_out = jnp.dot(expert_act, expert_down[0], preferred_element_type=jnp.float32).reshape(
        dp_count, capacity, model_width
    )
    returned = (
        lax.all_to_all(
            expert_out.astype(jnp.bfloat16), "dp", split_axis=0, concat_axis=0, tiled=True
        )
        .astype(expert_out.dtype)
        .reshape(dp_count * capacity, model_width)
    )
    picked_out = jnp.take(returned, target, axis=0).reshape(group_rows, top_count, model_width)
    moe_part = shared_out + jnp.sum(picked_out, axis=1)
    moe = lax.psum_scatter(
        moe_part.reshape(hid_count, item_count, local_len, model_width).astype(jnp.bfloat16),
        "hid",
        scatter_dimension=0,
        tiled=True,
    ).astype(jnp.float32)[0]
    output = (residual + gate_mid * moe).astype(jnp.bfloat16)
    grad_out = cotangent.astype(jnp.float32)
    grad_gate_mid = jnp.sum(grad_out * moe, axis=1)
    grad_moe = (gate_mid * grad_out).astype(jnp.bfloat16)
    grad_all = lax.all_gather(grad_moe[None], "hid", axis=0, tiled=True).reshape(
        group_rows, model_width
    )
    grad_shared_act = jnp.dot(grad_all, shared_down.T, preferred_element_type=jnp.float32)
    grad_shared_pre = gelu_back(shared_pre, grad_shared_act).astype(jnp.bfloat16)
    shared_down_grad = jnp.dot(shared_act.T, grad_all, preferred_element_type=jnp.float32)
    shared_up_grad = jnp.dot(mid_rows.T, grad_shared_pre, preferred_element_type=jnp.float32)
    grad_mid_part = jnp.dot(grad_shared_pre, shared_up.T, preferred_element_type=jnp.float32)
    grads_pad = jnp.concatenate([grad_all, jnp.zeros((1, model_width), jnp.bfloat16)], axis=0)
    send_grads = jnp.take(grads_pad, token_of, axis=0).reshape(dp_count, capacity, model_width)
    expert_grads = lax.all_to_all(
        send_grads, "dp", split_axis=0, concat_axis=0, tiled=True
    ).reshape(slot_rows, model_width)
    grad_expert_act = jnp.dot(expert_grads, expert_down[0].T, preferred_element_type=jnp.float32)
    grad_gate_slot = jnp.sum(grad_expert_act * expert_gelu, axis=1)
    grad_expert_pre = gelu_back(expert_pre, grad_expert_act * gate_col).astype(jnp.bfloat16)
    expert_down_grad = jnp.dot(expert_act.T, expert_grads, preferred_element_type=jnp.float32)[None]
    expert_up_grad = jnp.dot(expert_rows.T, grad_expert_pre, preferred_element_type=jnp.float32)[
        None
    ]
    grad_slot_rows = jnp.dot(grad_expert_pre, expert_up[0].T, preferred_element_type=jnp.float32)
    slot_grad_rows = grad_slot_rows.reshape(dp_count, capacity, model_width)
    slot_grad_gates = grad_gate_slot.reshape(dp_count, capacity)
    back_rows, back_gates = (
        lax.all_to_all(slot_grad_rows, "dp", split_axis=0, concat_axis=0, tiled=True),
        lax.all_to_all(slot_grad_gates, "dp", split_axis=0, concat_axis=0, tiled=True),
    )
    grad_pair_rows = jnp.take(back_rows.reshape(dp_count * capacity, model_width), target, axis=0)
    grad_mid_part = grad_mid_part + jnp.sum(
        grad_pair_rows.reshape(group_rows, top_count, model_width), axis=1
    )
    grad_pair_gates = jnp.take(back_gates.reshape(-1), target).reshape(
        hid_count, item_count, local_len, top_count
    )
    grad_mid_own, grad_gates = (
        lax.psum_scatter(
            grad_mid_part.reshape(hid_count, item_count, local_len, model_width).astype(
                jnp.bfloat16
            ),
            "hid",
            scatter_dimension=0,
            tiled=True,
        ).astype(jnp.float32),
        lax.psum_scatter(
            grad_pair_gates.astype(jnp.bfloat16), "hid", scatter_dimension=0, tiled=True
        ).astype(jnp.float32),
    )
    grad_mid_own = grad_mid_own[0]
    grad_gates = grad_gates[0]
    grad_soft_gate = gate_soft * (
        grad_gates - jnp.sum(gate_soft * grad_gates, axis=-1, keepdims=True)
    )
    grad_logits = (
        jnp.sum(route_hot * grad_soft_gate[..., None], axis=2)
        .astype(jnp.bfloat16)
        .reshape(row_count, dp_count)
    )
    router_full_grad = jnp.dot(mid_own_rows.T, grad_logits, preferred_element_type=jnp.float32)
    grad_mid = grad_mid_own + jnp.dot(
        grad_logits, router_full.T, preferred_element_type=jnp.float32
    ).reshape(item_count, local_len, model_width)
    grad_scale_mid = jnp.sum(grad_mid * normed_mid, axis=1)
    grad_shift_mid = jnp.sum(grad_mid, axis=1)
    grad_residual = grad_out + norm_back(grad_mid * (1.0 + scale_mid), normed_mid, inverse_mid)
    grad_gate_in = jnp.sum(grad_residual * branch, axis=1)
    grad_branch = (gate_in * grad_residual).astype(jnp.bfloat16).reshape(row_count, model_width)
    out_full_grad = jnp.dot(attended.T, grad_branch, preferred_element_type=jnp.float32)
    grad_attended = jnp.dot(grad_branch, out_full.T, preferred_element_type=jnp.float32).astype(
        jnp.bfloat16
    )
    grad_attended = grad_attended.reshape(item_count, local_len, HEADS, HDIM)
    scores = masked_scores()
    soft = jnp.exp(scores - log_total)
    grad_soft = jnp.einsum(
        "iqhd,kilhd->ihqkl", grad_attended, value_rows, preferred_element_type=jnp.float32
    )
    grad_scores = (
        soft * (grad_soft - jnp.sum(soft * grad_soft, axis=(3, 4), keepdims=True))
    ).astype(jnp.bfloat16)
    grad_queries = (
        jnp.einsum("ihqkl,kilhd->iqhd", grad_scores, key_rows, preferred_element_type=jnp.float32)
        * head_scale
    )
    grad_keys = (
        jnp.einsum("ihqkl,iqhd->kilhd", grad_scores, queries, preferred_element_type=jnp.float32)
        * head_scale
    )
    grad_values = jnp.einsum(
        "ihqkl,iqhd->kilhd",
        soft.astype(jnp.bfloat16),
        grad_attended,
        preferred_element_type=jnp.float32,
    )
    grad_kv = jnp.concatenate(
        [
            grad_keys.reshape(hid_count, item_count, local_len, model_width),
            grad_values.reshape(hid_count, item_count, local_len, model_width),
        ],
        axis=-1,
    )
    grad_kv_own = lax.psum_scatter(
        grad_kv.astype(jnp.bfloat16), "hid", scatter_dimension=0, tiled=True
    ).astype(jnp.float32)[0]
    grad_projected = jnp.concatenate(
        [grad_queries.reshape(item_count, local_len, model_width), grad_kv_own], axis=-1
    )
    grad_projected = grad_projected.astype(jnp.bfloat16).reshape(row_count, 3 * model_width)
    qkv_full_grad = jnp.dot(in_rows.T, grad_projected, preferred_element_type=jnp.float32)
    grad_in = jnp.dot(grad_projected, qkv_full.T, preferred_element_type=jnp.float32).reshape(
        item_count, local_len, model_width
    )
    grad_scale_in = jnp.sum(grad_in * normed_in, axis=1)
    grad_shift_in = jnp.sum(grad_in, axis=1)
    tokens_grad = grad_residual + norm_back(grad_in * (1.0 + scale_in), normed_in, inverse_in)
    grad_shifts = jnp.stack(
        [grad_shift_in, grad_scale_in, grad_gate_in, grad_shift_mid, grad_scale_mid, grad_gate_mid],
        axis=1,
    )
    grad_shifts = grad_shifts.reshape(item_count, 6 * model_width)
    modulation_part = exact_dot(scaled.astype(jnp.float32).T, grad_shifts)
    grad_cond = silu_back(cond, exact_dot(grad_shifts, modulation_full.T))
    time_part = exact_dot(time_hot.astype(jnp.float32).T, grad_cond)
    class_part = exact_dot(class_hot.astype(jnp.float32).T, grad_cond)
    shard_grads = (
        lax.psum_scatter(
            qkv_full_grad.astype(jnp.bfloat16), "hid", scatter_dimension=0, tiled=True
        ).astype(jnp.float32),
        lax.psum_scatter(
            out_full_grad.astype(jnp.bfloat16), "hid", scatter_dimension=0, tiled=True
        ).astype(jnp.float32),
        lax.psum_scatter(
            router_full_grad.astype(jnp.bfloat16), "hid", scatter_dimension=0, tiled=True
        ).astype(jnp.float32),
        lax.psum_scatter(
            modulation_part.astype(jnp.bfloat16), "hid", scatter_dimension=0, tiled=True
        ).astype(jnp.float32),
        lax.psum_scatter(
            time_part.astype(jnp.bfloat16), "hid", scatter_dimension=0, tiled=True
        ).astype(jnp.float32),
        lax.psum_scatter(
            class_part.astype(jnp.bfloat16), "hid", scatter_dimension=0, tiled=True
        ).astype(jnp.float32),
    )
    qkv_shard, out_shard, router_shard, modulation_shard, time_shard, class_shard = shard_grads
    summed = (
        lax.psum(qkv_shard.astype(jnp.bfloat16), "dp").astype(jnp.float32),
        lax.psum(out_shard.astype(jnp.bfloat16), "dp").astype(jnp.float32),
        lax.psum(router_shard.astype(jnp.bfloat16), "dp").astype(jnp.float32),
        lax.psum(modulation_shard.astype(jnp.bfloat16), "dp").astype(jnp.float32),
        lax.psum(time_shard.astype(jnp.bfloat16), "dp").astype(jnp.float32),
        lax.psum(class_shard.astype(jnp.bfloat16), "dp").astype(jnp.float32),
        lax.psum(shared_up_grad.astype(jnp.bfloat16), "dp").astype(jnp.float32),
        lax.psum(shared_down_grad.astype(jnp.bfloat16), "dp").astype(jnp.float32),
    )
    return (
        output,
        tokens_grad,
        summed[4],
        summed[5],
        summed[3],
        summed[0],
        summed[1],
        summed[2],
        summed[6],
        summed[7],
        expert_up_grad,
        expert_down_grad,
    )


def solution(mesh):
    placed = (
        P("dp", "hid", None),
        P("dp", "hid", None),
        P("dp"),
        P("dp"),
        P("dp"),
        P("dp", None, None),
        P("hid", None),
        P("hid", None),
        P("hid", None),
        P("hid", None),
        P("hid", None),
        P("hid", None),
        P(None, "hid"),
        P("hid", None),
        P("dp", None, "hid"),
        P("dp", "hid", None),
    )
    return jax.shard_map(
        shards,
        mesh=mesh,
        in_specs=placed,
        out_specs=(
            P("dp", "hid", None),
            P("dp", "hid", None),
            P("hid", None),
            P("hid", None),
            P("hid", None),
            P("hid", None),
            P("hid", None),
            P("hid", None),
            P(None, "hid"),
            P("hid", None),
            P("dp", None, "hid"),
            P("dp", "hid", None),
        ),
        check_vma=False,
    )
```

profile of v0, /device:TPU:0, one launch (start us, length us, event | category | flops | bytes accessed | tf_op | source)
XLA Modules:
  0.0 1375.1 jit_solution(16028447857429717611)
XLA Ops:
  11.8 37.5 %all-gather.27.cloned.1.call-done = bf16[4,250,768]{2,1,0:T(8,128)(2,1)} async-done(((bf16[1,250,768]{2,1,0:T(8,128)(2,1)}), bf16[4,250,768]{2,1,0:T(8,128)(2,1)}) %all-gather.27.cloned.1.call-update) | async-done | bytes 1536016 | tf_op jit(solution)/shard_map/all_gather | solution.py:72
  51.2 35.7 %all-gather.29.cloned.1.call-done = bf16[4,250,768]{2,1,0:T(8,128)(2,1)} async-done(((bf16[1,250,768]{2,1,0:T(8,128)(2,1)}), bf16[4,250,768]{2,1,0:T(8,128)(2,1)}) %all-gather.29.cloned.1.call-update) | async-done | bytes 1536016 | tf_op jit(solution)/shard_map/all_gather | solution.py:73
  92.5 123.0 %all-gather.15.cloned.1.call-done = bf16[768,4608]{1,0:T(8,128)(2,1)} async-done(((bf16[192,4608]{1,0:T(8,128)(2,1)}), bf16[768,4608]{1,0:T(8,128)(2,1)}) %all-gather.15.cloned.1.call-update) | async-done | bytes 7077904 | tf_op jit(solution)/shard_map/all_gather | solution.py:71
  215.5 10.4 copy.128
  225.9 4.9 fusion.112
  231.5 53.6 %all-gather.17.cloned.1.call-done = bf16[768,2304]{1,0:T(8,128)(2,1)} async-done(((bf16[192,2304]{1,0:T(8,128)(2,1)}), bf16[768,2304]{1,0:T(8,128)(2,1)}) %all-gather.17.cloned.1.call-update) | async-done | bytes 3538960 | tf_op jit(solution)/shard_map/all_gather | solution.py:68
  298.1 54.4 %all-gather.21.cloned.1.call-done = bf16[4,256,1536]{2,1,0:T(8,128)(2,1)} async-done(((bf16[1,256,1536]{2,1,0:T(8,128)(2,1)}), bf16[4,256,1536]{2,1,0:T(8,128)(2,1)}) %all-gather.21.cloned.1.call-update) | async-done | bytes 3145744 | tf_op jit(solution)/shard_map/all_gather | solution.py:103
  366.9 9.8 fusion.9
  387.4 13.5 all-gather.5
  402.3 8.1 scatter_custom_fusion
  410.4 10.9 all-gather.25.cloned.1.call-done
  422.9 8.5 gather_fusion.4
  432.4 9.3 all_gather.38
  442.2 15.4 %gather_fusion = bf16[2560]{0:T(1024)(128)(2,1)S(1)} fusion(bf16[2049]{0:T(1024)(128)(2,1)S(1)} %pad_maximum_fusion.4, s32[3072]{0:T(1024)S(1)} %pad_clamp_fusion.1), kind=kCustom, calls=%fused_computation.4 | custom fusion | bytes 20480 | tf_op jit(solution)/shard_map/jit(_take)/gather | solution.py:175
  464.9 8.6 gather_fusion.2
  473.5 5.9 broadcast_select_fusion
  479.4 50.7 %all_to_all.35 = bf16[8,320,768]{2,1,0:T(8,128)(2,1)} all-to-all(bf16[8,320,768]{2,1,0:T(8,128)(2,1)} %bitcast.261), channel_id=1, replica_groups=mesh['dp'=8,'hid'=4] {'dp'}, dimensions={0} | all-to-all | bytes 7864320 | tf_op jit(solution)/shard_map/all_to_all | solution.py:177
  535.0 8.4 fusion.47
  543.4 37.7 %all-to-all-done.3 = bf16[8,320,768]{2,1,0:T(8,128)(2,1)} async-done(((bf16[8,320,768]{2,1,0:T(8,128)(2,1)}), bf16[8,320,768]{2,1,0:T(8,128)(2,1)}, u32[]{:S(2)}, u32[]{:S(2)}) %all-to-all-start.3) | async-done | bytes 3932192 | tf_op jit(solution)/shard_map/all_to_all | solution.py:218
  581.1 13.8 %multiply_reduce_fusion.1 = (f32[2560]{0:T(1024)S(1)}, bf16[2560,768]{1,0:T(8,128)(2,1)}, bf16[2560,768]{1,0:T(8,128)(2,1)S(1)}) fusion(f32[2560,768]{1,0:T(8,128)} %fusion.47, f32[2560]{0:T(1024)S(1)} %reshape.949, bf16[2560,768]{1,0:T(8,128)(2,1)} %bitcast.42, bf16[1,768,768]{2,1,0:T(8,128)(2,1)S(1)} %copy-done), kind=kOutput, calls=%fused_computation.24 | convolution fusion | flops 3078878720 | bytes 20860928 | tf_op jit(solution)/shard_map/dot_general | solution.py:221
  606.2 8.5 fusion.42
  614.7 37.8 %all-to-all-done.2 = bf16[8,320,768]{2,1,0:T(8,128)(2,1)} async-done(((bf16[8,320,768]{2,1,0:T(8,128)(2,1)}), bf16[8,320,768]{2,1,0:T(8,128)(2,1)}, u32[]{:S(2)}, u32[]{:S(2)}) %all-to-all-start.2) | async-done | bytes 3932192 | tf_op jit(solution)/shard_map/all_to_all | solution.py:190
  665.0 6.4 bitcast_convert_fusion
  671.4 13.9 %gather_fusion.3 = f32[2048,768]{1,0:T(8,128)} fusion(f32[2560,768]{1,0:T(8,128)} %bitcast_convert_fusion, s32[2048]{0:T(1024)S(1)} %copy-done.55), kind=kCustom, calls=%fused_computation.1.clone | custom fusion | bytes 12591104 | tf_op jit(solution)/shard_map/jit(_take)/gather | solution.py:196
  685.3 60.5 %all-to-all-done.4 = f32[8,320,768]{2,1,0:T(8,128)} async-done(((f32[8,320,768]{2,1,0:T(8,128)}), f32[8,320,768]{2,1,0:T(8,128)}, u32[]{:S(2)}, u32[]{:S(2)}) %all-to-all-start.4) | async-done | bytes 7864352 | tf_op jit(solution)/shard_map/all_to_all | solution.py:232
  745.8 13.9 %gather_fusion.5 = f32[2048,768]{1,0:T(8,128)} fusion(f32[2560,768]{1,0:T(8,128)} %bitcast.45, s32[2048]{0:T(1024)S(1)} %copy-done.55), kind=kCustom, calls=%fused_computation.3.clone | custom fusion | bytes 12591104 | tf_op jit(solution)/shard_map/jit(_take)/gather | solution.py:235
  759.8 8.6 broadcast_select_fusion.2
  768.3 8.5 reshape.942
  776.9 12.0 reduce_sum.230
  793.5 8.4 reshape.937
  801.9 12.1 reduce_sum.229
  814.0 6.1 add_convert_fusion.1
  829.0 13.3 gather_fusion.1
  843.0 10.0 all-reduce.2
  856.2 6.8 reduce-scatter.14.cloned.1.call-done
  867.3 4.9 fusion.25
  872.3 10.2 multiply_reduce_fusion
  882.8 6.9 multiply_convert_fusion.1
  901.3 52.5 %reduce-scatter.18.cloned.1.call-done = bf16[1,1,256,1536]{2,3,0,1:T(8,128)(2,1)} async-done(((bf16[4,1,256,1536]{2,3,0,1:T(8,128)(2,1)}), bf16[1,1,256,1536]{2,3,0,1:T(8,128)(2,1)}) %reduce-scatter.18.cloned.1.call-update) | async-done | bytes 786448 | tf_op jit(solution)/shard_map/reduce_scatter | solution.py:308
  973.9 5.0 convolution_convert_fusion.4
  978.9 5.6 convolution_reduce_fusion
  986.0 105.3 %fusion.107 = (bf16[256,768]{1,0:T(8,128)(2,1)S(1)}, bf16[256,768]{1,0:T(8,128)(2,1)}) fusion(bf16[1000,768]{1,0:T(8,128)(2,1)} %get-tuple-element.58, bf16[1000,768]{1,0:T(8,128)(2,1)S(1)} %get-tuple-element.57), kind=kCustom, calls=%all-reduce-scatter.2 | all-reduce-scatter fusion | flops 1572865 | bytes 3858944
  1092.1 7.8 collective-permute-start.1
  1111.3 116.1 %reduce-scatter.20.cloned.1.call-done = bf16[192,4608]{1,0:T(8,128)(2,1)} async-done(((bf16[768,4608]{1,0:T(8,128)(2,1)}), bf16[192,4608]{1,0:T(8,128)(2,1)}) %reduce-scatter.20.cloned.1.call-update) | async-done | bytes 1769488 | tf_op jit(solution)/shard_map/reduce_scatter | solution.py:341
  1227.4 8.1 convolution_bitcast_fusion
  1240.4 9.8 reduce-scatter.26.cloned.1.call-done
  1251.0 11.9 psum.61
  1264.7 91.2 %all-reduce.11.cloned.1.call-done = (bf16[250,768]{1,0:T(8,128)(2,1)}, bf16[250,768]{1,0:T(8,128)(2,1)}, bf16[192,4608]{1,0:T(8,128)(2,1)}, bf16[192,2304]{1,0:T...) async-done(((bf16[250,768]{1,0:T(8,128)(2,1)}, bf16[250,768]{1,0:T(8,128)(2,1)}, bf16[192,4608]{1,0:T(8,128)(2,1)}, ...) | async-done | bytes 6076432 | tf_op jit(solution)/shard_map/psum | solution.py:357
  (391 shorter events, 174.5 us)
Async XLA Ops:
  7.2 573.9 %copy-start = (bf16[1,768,768]{2,1,0:T(8,128)(2,1)S(1)}, bf16[1,768,768]{2,1,0:T(8,128)(2,1)}, u32[]{:S(2)}) copy-start(bf16[1,768,768]{2,1,0:T(8,128)(2,1)} %param.35) | copy-start | bytes 3538948
  7.2 42.2 %all-gather.27.cloned.1.call-start = ((), (), s32[]{:S(2)}) async-start(), calls=%async_computation.25 | async-start | bytes 1966080 | tf_op jit(solution)/shard_map/all_gather | solution.py:72
  7.9 78.9 %all-gather.29.cloned.1.call-start = ((), (), s32[]{:S(2)}) async-start(), calls=%async_computation.26 | async-start | bytes 1966080 | tf_op jit(solution)/shard_map/all_gather | solution.py:73
  8.7 206.8 %all-gather.15.cloned.1.call-start = ((), (), s32[]{:S(2)}) async-start(), calls=%async_computation.13 | async-start | bytes 8847360 | tf_op jit(solution)/shard_map/all_gather | solution.py:71
  9.4 275.7 %all-gather.17.cloned.1.call-start = ((), (), s32[]{:S(2)}) async-start(), calls=%async_computation.14 | async-start | bytes 4423680 | tf_op jit(solution)/shard_map/all_gather | solution.py:68
  10.0 342.5 %all-gather.21.cloned.1.call-start = ((), (), s32[]{:S(2)}) async-start(), calls=%async_computation.22 | async-start | bytes 3932160 | tf_op jit(solution)/shard_map/all_gather | solution.py:103
  11.5 273.5 %copy-start.64 = (f32[256]{0:T(256)}, f32[256]{0:T(256)S(1)}, u32[]{:S(2)}) copy-start(f32[256]{0:T(256)S(1)} %broadcast_multiply_fusion.6) | copy-start | bytes 3076
  11.8 273.3 %copy-start.74 = (f32[256]{0:T(256)}, f32[256]{0:T(256)S(1)}, u32[]{:S(2)}) copy-start(f32[256]{0:T(256)S(1)} %add_rsqrt_fusion.1) | copy-start | bytes 3076
  231.4 56.8 %copy-start.39 = (f32[768]{0:T(1024)}, f32[768]{0:T(1024)S(1)}, u32[]{:S(2)}) copy-start(f32[768]{0:T(1024)S(1)} %get-tuple-element.26) | copy-start | bytes 9220
  231.4 56.8 %copy-start.43 = (f32[768]{0:T(1024)}, f32[768]{0:T(1024)S(1)}, u32[]{:S(2)}) copy-start(f32[768]{0:T(1024)S(1)} %get-tuple-element.25) | copy-start | bytes 9220
  231.4 65.2 %copy-start.60 = (f32[768]{0:T(1024)}, f32[768]{0:T(1024)S(1)}, u32[]{:S(2)}) copy-start(f32[768]{0:T(1024)S(1)} %get-tuple-element.22) | copy-start | bytes 9220
  231.4 151.4 %copy-start.56 = (f32[768]{0:T(1024)}, f32[768]{0:T(1024)S(1)}, u32[]{:S(2)}) copy-start(f32[768]{0:T(1024)S(1)} %get-tuple-element.27) | copy-start | bytes 9220
  231.5 154.3 %copy-start.45 = (f32[768]{0:T(1024)}, f32[768]{0:T(1024)S(1)}, u32[]{:S(2)}) copy-start(f32[768]{0:T(1024)S(1)} %get-tuple-element.24) | copy-start | bytes 9220
  290.3 92.5 %all-gather.19.cloned.1.call-start = ((), (), s32[]{:S(2)}) async-start(), calls=%async_computation.15 | async-start | bytes 1474560 | tf_op jit(solution)/shard_map/all_gather | solution.py:69
  290.9 130.5 %all-gather.25.cloned.1.call-start = ((), (), s32[]{:S(2)}) async-start(), calls=%async_computation.24 | async-start | bytes 1966080 | tf_op jit(solution)/shard_map/all_gather | solution.py:208
  295.8 61.3 %copy-start.51 = (s32[2048]{0:T(1024)}, s32[2048]{0:T(1024)S(1)}, u32[]{:S(2)}) copy-start(s32[2048]{0:T(1024)S(1)} %fusion.80) | copy-start | bytes 24580
  296.6 62.6 %copy-start.15 = (bf16[1,256,768]{1,2,0:T(8,128)(2,1)}, bf16[1,256,768]{1,2,0:T(8,128)(2,1)S(1)}, u32[]{:S(2)}) copy-start(bf16[1,256,768]{1,2,0:T(8,128)(2,1)S(1)} %copy.130) | copy-start | bytes 1179652
  297.5 165.9 %all-gather.23.cloned.1.call-start = ((), (), s32[]{:S(2)}) async-start(), calls=%async_computation.23 | async-start | bytes 1966080 | tf_op jit(solution)/shard_map/all_gather | solution.py:147
  459.6 19.8 %all-to-all-start = ((bf16[8,2,160]{2,1,0:T(2,128)(2,1)}), bf16[8,2,160]{2,1,0:T(2,128)(2,1)S(1)}, u32[]{:S(2)}, u32[]{:S(2)}) async-start(bf16[8,2,160]{2,1,0:T(2,128)(2,1)} %reshape.1068), calls=%async_computation | async-start | bytes 16384 | tf_op jit(solution)/shard_map/all_to_all | solution.py:178
  530.1 51.0 %all-to-all-start.3 = ((bf16[8,320,768]{2,1,0:T(8,128)(2,1)}), bf16[8,320,768]{2,1,0:T(8,128)(2,1)}, u32[]{:S(2)}, u32[]{:S(2)}) async-start(bf16[8,320,768]{2,1,0:T(8,128)(2,1)} %bitcast.260), calls=%async_computation.4 | async-start | bytes 7864320 | tf_op jit(solution)/shard_map/all_to_all | solution.py:218
  601.5 51.0 %all-to-all-start.2 = ((bf16[8,320,768]{2,1,0:T(8,128)(2,1)}), bf16[8,320,768]{2,1,0:T(8,128)(2,1)}, u32[]{:S(2)}, u32[]{:S(2)}) async-start(bf16[8,320,768]{2,1,0:T(8,128)(2,1)} %convolution_convert_fusion.2), calls=%async_computation.2 | async-start | bytes 7864320 | tf_op jit(solution)/shard_map/all_to_all | solution.py:190
  614.7 42.7 %copy-start.52 = (s32[2048]{0:T(1024)S(1)}, s32[2048]{0:T(1024)}, u32[]{:S(2)}) copy-start(s32[2048]{0:T(1024)} %copy-done.51) | copy-start | bytes 24580
  614.7 42.8 %copy-start.25 = (bf16[4,256,768]{2,1,0:T(8,128)(2,1)S(1)}, bf16[4,256,768]{2,1,0:T(8,128)(2,1)}, u32[]{:S(2)}) copy-start(bf16[4,256,768]{2,1,0:T(8,128)(2,1)} %all-gather.25.cloned.1.call-done) | copy-start | bytes 4718596
  652.5 93.3 %all-to-all-start.4 = ((f32[8,320,768]{2,1,0:T(8,128)}), f32[8,320,768]{2,1,0:T(8,128)}, u32[]{:S(2)}, u32[]{:S(2)}) async-start(f32[8,320,768]{2,1,0:T(8,128)} %fusion.42), calls=%async_computation.5 | async-start | bytes 15728640 | tf_op jit(solution)/shard_map/all_to_all | solution.py:232
  657.4 197.0 %reduce-scatter.16.cloned.1.call-start = ((), (), s32[]{:S(2)}) async-start(), calls=%async_computation.17 | async-start | bytes 1966080 | tf_op jit(solution)/shard_map/reduce_scatter | solution.py:243
  665.0 123.9 %copy-start.93 = (bf16[1024,768]{1,0:T(8,128)(2,1)}, bf16[1024,768]{1,0:T(8,128)(2,1)S(1)}, u32[]{:S(2)}) copy-start(bf16[1024,768]{1,0:T(8,128)(2,1)S(1)} %get-tuple-element.68) | copy-start | bytes 4718596
  793.4 69.5 %reduce-scatter.14.cloned.1.call-start = ((), (), s32[]{:S(2)}) async-start(), calls=%async_computation.16 | async-start | bytes 1966080 | tf_op jit(solution)/shard_map/reduce_scatter | solution.py:198
  820.1 34.3 %copy-start.5 = (f32[1,256,768]{2,1,0:T(8,128)S(1)}, f32[1,256,768]{2,1,0:T(8,128)}, u32[]{:S(2)}) copy-start(f32[1,256,768]{2,1,0:T(8,128)} %copy-done.4) | copy-start | bytes 2359300
  820.1 34.3 %copy-start.42 = (bf16[768,8]{0,1:T(8,128)(2,1)S(1)}, bf16[768,8]{0,1:T(8,128)(2,1)}, u32[]{:S(2)}) copy-start(bf16[768,8]{0,1:T(8,128)(2,1)} %reshape.1025) | copy-start | bytes 36868
  820.1 34.3 %copy-start.46 = (f32[768]{0:T(1024)S(1)}, f32[768]{0:T(1024)}, u32[]{:S(2)}) copy-start(f32[768]{0:T(1024)} %copy-done.45) | copy-start | bytes 9220
  820.2 34.3 %copy-start.67 = (f32[256]{0:T(256)S(1)}, f32[256]{0:T(256)}, u32[]{:S(2)}) copy-start(f32[256]{0:T(256)} %copy-done.66) | copy-start | bytes 3076
  820.2 34.3 %copy-start.77 = (f32[256]{0:T(256)S(1)}, f32[256]{0:T(256)}, u32[]{:S(2)}) copy-start(f32[256]{0:T(256)} %copy-done.76) | copy-start | bytes 3076
  820.9 8.0 all-to-all-start.5
  824.2 129.5 %reduce-scatter.18.cloned.1.call-start = ((), (), s32[]{:S(2)}) async-start(), calls=%async_computation.18 | async-start | bytes 3932160 | tf_op jit(solution)/shard_map/reduce_scatter | solution.py:308
  894.3 217.0 %reduce-scatter.24.cloned.1.call-start = ((), (), s32[]{:S(2)}) async-start(), calls=%async_computation.21 | async-start | bytes 1474560 | tf_op jit(solution)/shard_map/reduce_scatter | solution.py:335
  896.8 57.0 %copy-start.7 = (bf16[1,256,768]{2,1,0:T(8,128)(2,1)S(1)}, bf16[1,256,768]{2,1,0:T(8,128)(2,1)}, u32[]{:S(2)}) copy-start(bf16[1,256,768]{2,1,0:T(8,128)(2,1)} %param.20) | copy-start | bytes 1179652
  896.8 56.9 %copy-start.40 = (f32[768]{0:T(1024)S(1)}, f32[768]{0:T(1024)}, u32[]{:S(2)}) copy-start(f32[768]{0:T(1024)} %copy-done.39) | copy-start | bytes 9220
  896.8 56.9 %copy-start.44 = (f32[768]{0:T(1024)S(1)}, f32[768]{0:T(1024)}, u32[]{:S(2)}) copy-start(f32[768]{0:T(1024)} %copy-done.43) | copy-start | bytes 9220
  896.8 56.9 %copy-start.65 = (f32[256]{0:T(256)S(1)}, f32[256]{0:T(256)}, u32[]{:S(2)}) copy-start(f32[256]{0:T(256)} %copy-done.64) | copy-start | bytes 3076
  896.8 56.9 %copy-start.75 = (f32[256]{0:T(256)S(1)}, f32[256]{0:T(256)}, u32[]{:S(2)}) copy-start(f32[256]{0:T(256)} %copy-done.74) | copy-start | bytes 3076
  896.8 214.4 %reduce-scatter.22.cloned.1.call-start = ((), (), s32[]{:S(2)}) async-start(), calls=%async_computation.20 | async-start | bytes 4423680 | tf_op jit(solution)/shard_map/reduce_scatter | solution.py:332
  901.3 56.7 %copy-start.33 = (bf16[12,64,256]{2,1,0:T(8,128)(2,1)}, bf16[12,64,256]{2,1,0:T(8,128)(2,1)S(1)}, u32[]{:S(2)}) copy-start(bf16[12,64,256]{2,1,0:T(8,128)(2,1)S(1)} %fusion.36) | copy-start | bytes 1179652
  958.0 269.3 %reduce-scatter.20.cloned.1.call-start = ((), (), s32[]{:S(2)}) async-start(), calls=%async_computation.19 | async-start | bytes 8847360 | tf_op jit(solution)/shard_map/reduce_scatter | solution.py:341
  968.4 281.7 %reduce-scatter.26.cloned.1.call-start = ((), (), s32[]{:S(2)}) async-start(), calls=%async_computation.27 | async-start | bytes 245760
  984.5 115.4 %copy-start.9 = (bf16[1,256,768]{2,1,0:T(8,128)(2,1)S(1)}, bf16[1,256,768]{2,1,0:T(8,128)(2,1)}, u32[]{:S(2)}) copy-start(bf16[1,256,768]{2,1,0:T(8,128)(2,1)} %add_convert_fusion.2) | copy-start | bytes 1179652
  1092.1 13.4 collective-permute-start.1
  1100.9 255.0 %all-reduce.11.cloned.1.call-start = ((), (), s32[]{:S(2)}) async-start(), calls=%async_computation.28 | async-start | bytes 12189696 | tf_op jit(solution)/shard_map/psum | solution.py:357
  1101.0 7.9 collective-permute-start
  (75 other events, 789.7 us)
Sparse Core Ops, SparseCore 0:
  9.6 39.7 all-gather.26
  50.9 35.8 all-gather.28
  88.4 127.0 all-gather.14
  216.9 68.0 all-gather.16
  290.4 62.0 all-gather.20
  353.9 28.8 all-gather.18
  385.0 36.3 all-gather.24
  423.5 35.9 all-gather.22
  793.5 32.0 reduce-scatter.15
  828.4 34.5 reduce-scatter.13
  894.4 59.2 reduce-scatter.17
  956.5 29.2 reduce-scatter.23
  988.6 111.7 reduce-scatter.21
  1102.6 124.6 reduce-scatter.19
  1230.0 20.0 reduce-scatter.25
  1255.4 100.4 all-reduce.10
where the time goes:
time: 1380 us
  waiting for transfers between devices  736 us (53%)
  blocking collectives  201 us (15%)
  local copies, waits for them, and re-layouts  149 us (11%)
  matrix products  136 us (10%)
  other arithmetic  99.9 us (7%)
  starting transfers between devices  35.3 us (3%)
  between operations  18.4 us (1%)
    all_gather x1, waiting for transfers between devices, shards(): lax.all_gather(modulation, 'hid', axis=0, tiled=True)  123 us
    reduce_scatter x1, waiting for transfers between devices, shards(): lax.psum_scatter(modulation_part.astype(jnp.bfloat16), 'hid', scatter_dim...  116 us
    unnamed x2, blocking collectives  115 us
    psum x1, waiting for transfers between devices, shards(): lax.psum(time_shard.astype(jnp.bfloat16), 'dp').astype(jnp.float32)  91.2 us
    all_to_all x1, waiting for transfers between devices, shards(): lax.all_to_all(slot_grad_rows, 'dp', split_axis=0, concat_axis=0, tiled=T...  60.5 us
    all_gather x1, waiting for transfers between devices, shards(): lax.all_gather(projected[None, :, :, model_width:], 'hid', axis=0, tiled=...  54.4 us
    all_gather x1, waiting for transfers between devices, shards(): lax.all_gather(qkv_weight, 'hid', axis=0, tiled=True)  53.6 us
    reduce_scatter x1, waiting for transfers between devices, shards(): lax.psum_scatter(grad_kv.astype(jnp.bfloat16), 'hid', scatter_dimension=0...  52.5 us
  transfers between devices with their start and end apart: 23, of which 16 were waited for; matrix products, arithmetic and copies ran while one was open for 27% of the time, Pallas kernels for 0%

commit v1 on v0

v1 whole, which is shorter than its diff:
```python
import functools

import jax
import jax.numpy as jnp
from jax import lax
from jax.experimental import pallas as pl
from jax.experimental.pallas import tpu as pltpu
from jax.sharding import PartitionSpec as P

HEADS = 12
HDIM = 64
F32 = jnp.float32
BF16 = jnp.bfloat16
MASKED = -1e30


def layer_norm(values):
    center = values - jnp.mean(values, axis=-1, keepdims=True)
    inverse = lax.rsqrt(jnp.mean(center * center, axis=-1, keepdims=True) + 1e-06)
    return (center * inverse, inverse)


def norm_back(grad_norm, normed, inverse):
    first = jnp.mean(grad_norm, axis=-1, keepdims=True)
    second = jnp.mean(grad_norm * normed, axis=-1, keepdims=True)
    return inverse * (grad_norm - first - normed * second)


def gelu_pair(values):
    square = values * values
    tanh = jnp.tanh(0.7978845608028654 * (values + 0.044715 * values * square))
    half = 0.5 * (1.0 + tanh)
    slope = half + 0.5 * values * (1.0 - tanh * tanh) * (
        0.7978845608028654 * (1.0 + 3.0 * 0.044715 * square)
    )
    return values * half, slope


def silu_back(cond, grad_out):
    return jax.vjp(jax.nn.silu, cond)[1](grad_out)[0]


def exact_dot(left, right):
    return jnp.dot(left, right, precision=lax.Precision.HIGHEST, preferred_element_type=F32)


def dot(left, right):
    return jnp.dot(left, right, preferred_element_type=F32)


def dot_t(left, right):
    return lax.dot_general(left, right, (((1,), (1,)), ((), ())), preferred_element_type=F32)


def t_dot(left, right):
    return lax.dot_general(left, right, (((0,), (0,)), ((), ())), preferred_element_type=F32)


def exchange(values, axis):
    return lax.all_to_all(values, axis, split_axis=0, concat_axis=0, tiled=True)


def copies(values, axis):
    count = lax.axis_size(axis)
    return exchange(jnp.broadcast_to(values[None], (count,) + values.shape), axis)


def small_sum(values, axis):
    return jnp.sum(copies(values, axis), axis=0)


def attend_kernel(length_ref, query_ref, all_ref, out_ref, log_ref, *, heads):
    cols = heads * HDIM
    item = pl.program_id(0)
    queries = query_ref.shape[1]
    full = all_ref.shape[1]
    valid = lax.broadcasted_iota(jnp.int32, (full, queries), 0) < length_ref[item]
    mixed = []
    logs = []
    for head in range(heads):
        at = head * HDIM
        query = query_ref[0, :, at : at + HDIM]
        key = all_ref[0, :, cols + at : cols + at + HDIM]
        value = all_ref[0, :, 2 * cols + at : 2 * cols + at + HDIM]
        scores = jnp.where(valid, dot_t(key, query) * HDIM ** (-0.5), MASKED)
        top = jnp.max(scores, axis=0, keepdims=True)
        terms = jnp.exp(scores - top)
        total = jnp.sum(terms, axis=0, keepdims=True)
        soft = (terms * (1.0 / total)).astype(BF16)
        mixed.append(t_dot(value, soft))
        logs.append(top + jnp.log(total))
    out_ref[0] = jnp.concatenate(mixed, axis=0).T.astype(BF16)
    log_ref[0] = jnp.concatenate(logs + [logs[0]] * (8 - heads), axis=0)


def attend_back_kernel(
    length_ref, query_ref, grad_ref, all_ref, log_ref, out_ref, key_acc, value_acc, *, heads
):
    cols = heads * HDIM
    item = pl.program_id(0)
    step = pl.program_id(1)
    queries = query_ref.shape[1]
    full = all_ref.shape[1]
    valid = lax.broadcasted_iota(jnp.int32, (full, queries), 0) < length_ref[item]

    @pl.when(step == 0)
    def _():
        key_acc[...] = jnp.zeros_like(key_acc)
        value_acc[...] = jnp.zeros_like(value_acc)

    query_grads = []
    for head in range(heads):
        at = head * HDIM
        query = query_ref[0, :, at : at + HDIM]
        grad = grad_ref[0, :, at : at + HDIM]
        key = all_ref[0, :, cols + at : cols + at + HDIM]
        value = all_ref[0, :, 2 * cols + at : 2 * cols + at + HDIM]
        scores = jnp.where(valid, dot_t(key, query) * HDIM ** (-0.5), MASKED)
        soft = jnp.exp(scores - log_ref[0, head : head + 1, :])
        grad_soft = dot_t(value, grad)
        mean = jnp.sum(soft * grad_soft, axis=0, keepdims=True)
        grad_scores = (soft * (grad_soft - mean)).astype(BF16)
        value_acc[head] += dot(soft.astype(BF16), grad)
        key_acc[head] += dot(grad_scores, query)
        query_grads.append(t_dot(key, grad_scores))
    grad_query = jnp.concatenate(query_grads, axis=0).T * HDIM ** (-0.5)
    out_ref[0, pl.ds(pl.multiple_of(step * queries, queries), queries), 0:cols] = grad_query.astype(BF16)

    @pl.when(step == pl.num_programs(1) - 1)
    def _():
        rest = [key_acc[head] * HDIM ** (-0.5) for head in range(heads)]
        rest += [value_acc[head] for head in range(heads)]
        out_ref[0, :, cols:] = jnp.concatenate(rest, axis=1).astype(BF16)


def attend(projected, lengths):
    items, full, three = projected.shape
    cols = three // 3
    heads = cols // HDIM
    queries = min(256, full)
    return pl.pallas_call(
        functools.partial(attend_kernel, heads=heads),
        grid_spec=pltpu.PrefetchScalarGridSpec(
            num_scalar_prefetch=1,
            grid=(items, full // queries),
            in_specs=[
                pl.BlockSpec((1, queries, three), lambda i, q, n: (i, q, 0)),
                pl.BlockSpec((1, full, three), lambda i, q, n: (i, 0, 0)),
            ],
            out_specs=[
                pl.BlockSpec((1, queries, cols), lambda i, q, n: (i, q, 0)),
                pl.BlockSpec((1, 8, queries), lambda i, q, n: (i, 0, q)),
            ],
        ),
        out_shape=[
            jax.ShapeDtypeStruct((items, full, cols), BF16),
            jax.ShapeDtypeStruct((items, 8, full), F32),
        ],
        name="attend",
    )(lengths, projected, projected)


def attend_back(projected, grad_attended, logs, lengths):
    items, full, three = projected.shape
    cols = three // 3
    heads = cols // HDIM
    queries = min(256, full)
    return pl.pallas_call(
        functools.partial(attend_back_kernel, heads=heads),
        grid_spec=pltpu.PrefetchScalarGridSpec(
            num_scalar_prefetch=1,
            grid=(items, full // queries),
            in_specs=[
                pl.BlockSpec((1, queries, three), lambda i, q, n: (i, q, 0)),
                pl.BlockSpec((1, queries, cols), lambda i, q, n: (i, q, 0)),
                pl.BlockSpec((1, full, three), lambda i, q, n: (i, 0, 0)),
                pl.BlockSpec((1, 8, queries), lambda i, q, n: (i, 0, q)),
            ],
            out_specs=pl.BlockSpec((1, full, three), lambda i, q, n: (i, 0, 0)),
            scratch_shapes=[
                pltpu.VMEM((heads, full, HDIM), F32),
                pltpu.VMEM((heads, full, HDIM), F32),
            ],
        ),
        out_shape=jax.ShapeDtypeStruct((items, full, three), BF16),
        name="attend_back",
    )(lengths, projected, grad_attended, projected, logs)


class HeadSplit:
    def __init__(self, tokens, qkv_weight, out_weight, lengths):
        self.hid = lax.axis_size("hid")
        self.items, self.local, self.width = tokens.shape
        self.cols = self.width // self.hid
        self.lengths = lengths
        own = qkv_weight.shape[0]
        parts = qkv_weight.reshape(own, 3, self.hid, self.cols).transpose(2, 0, 1, 3)
        self.qkv = exchange(parts.reshape(self.hid, own, 3 * self.cols), "hid").reshape(
            self.width, 3 * self.cols
        )
        self.out = lax.all_gather(out_weight, "hid", axis=0, tiled=True)
        tokens_all = lax.all_gather(tokens[None], "hid", axis=0, tiled=True)
        self.tokens_all = tokens_all.transpose(1, 0, 2, 3).reshape(
            self.items, self.hid * self.local, self.width
        )

    def to_heads(self, rows):
        parts = rows.reshape(self.items, self.local, self.hid, self.cols).transpose(2, 0, 1, 3)
        return (
            exchange(parts, "hid")
            .transpose(1, 0, 2, 3)
            .reshape(self.items, self.hid * self.local, self.cols)
        )

    def to_rows(self, columns):
        parts = columns.reshape(self.items, self.hid, self.local, self.cols).transpose(1, 0, 2, 3)
        return exchange(parts, "hid").transpose(1, 2, 0, 3).reshape(
            self.items * self.local, self.width
        )

    def forward(self, shift_in, scale_in):
        normed, _ = layer_norm(self.tokens_all.astype(F32))
        hidden = (normed * (1.0 + scale_in) + shift_in).astype(BF16)
        self.hidden = hidden.reshape(-1, self.width)
        self.projected = (
            dot(self.hidden, self.qkv).astype(BF16).reshape(self.items, -1, 3 * self.cols)
        )
        attended, self.logs = attend(self.projected, self.lengths)
        self.attended = self.to_rows(attended)
        return dot(self.attended, self.out)

    def backward(self, grad_branch):
        out_grad = t_dot(self.attended, grad_branch)
        grad_attended = dot_t(grad_branch, self.out).astype(BF16)
        grad_heads = self.to_heads(grad_attended.reshape(self.items, self.local, self.width))
        grad_projected = attend_back(self.projected, grad_heads, self.logs, self.lengths)
        rows = grad_projected.reshape(-1, 3 * self.cols)
        grad_part = dot_t(rows, self.qkv).astype(BF16)
        grad_part = grad_part.reshape(self.items, self.hid, self.local, self.width)
        grad_in = lax.psum_scatter(
            grad_part.transpose(1, 0, 2, 3), "hid", scatter_dimension=0, tiled=True
        )[0].astype(F32)
        qkv_grad = t_dot(self.hidden, rows)
        return grad_in, qkv_grad, out_grad

    def join_qkv(self, parts):
        chunk = parts.shape[1]
        return (
            parts.reshape(self.hid, chunk, 3, self.cols)
            .transpose(1, 2, 0, 3)
            .reshape(chunk, 3 * self.width)
        )


class PatchSplit:
    def __init__(self, tokens, qkv_weight, out_weight, lengths):
        self.hid = lax.axis_size("hid")
        self.items, self.local, self.width = tokens.shape
        self.tokens = tokens
        self.lengths = lengths
        self.qkv = lax.all_gather(qkv_weight, "hid", axis=0, tiled=True)
        self.out = lax.all_gather(out_weight, "hid", axis=0, tiled=True)

    def scores(self):
        positions = jnp.arange(self.hid * self.local, dtype=jnp.int32).reshape(
            self.hid, self.local
        )
        valid = (positions[None] < self.lengths[:, None, None])[:, None, None]
        raw = jnp.einsum("iqhd,kilhd->ihqkl", self.queries, self.keys, preferred_element_type=F32)
        return jnp.where(valid, raw * HDIM ** (-0.5), MASKED)

    def forward(self, shift_in, scale_in):
        items, local, width = self.items, self.local, self.width
        normed, _ = layer_norm(self.tokens.astype(F32))
        hidden = (normed * (1.0 + scale_in) + shift_in).astype(BF16)
        self.hidden = hidden.reshape(-1, width)
        projected = dot(self.hidden, self.qkv).astype(BF16).reshape(items, local, 3 * width)
        self.queries = projected[:, :, :width].reshape(items, local, HEADS, HDIM)
        gathered = lax.all_gather(projected[None, :, :, width:], "hid", axis=0, tiled=True)
        shape = (self.hid, items, local, HEADS, HDIM)
        self.keys = gathered[..., :width].reshape(shape)
        self.values = gathered[..., width:].reshape(shape)
        scores = self.scores()
        top = jnp.max(scores, axis=(3, 4), keepdims=True)
        total = jnp.sum(jnp.exp(scores - top), axis=(3, 4), keepdims=True)
        self.log_total = top + jnp.log(total)
        soft_low = jnp.exp(scores - self.log_total).astype(BF16)
        attended = jnp.einsum("ihqkl,kilhd->iqhd", soft_low, self.values, preferred_element_type=F32)
        self.attended = attended.astype(BF16).reshape(-1, width)
        return dot(self.attended, self.out)

    def backward(self, grad_branch):
        items, local, width = self.items, self.local, self.width
        out_grad = t_dot(self.attended, grad_branch)
        grad_attended = dot_t(grad_branch, self.out).astype(BF16)
        grad_attended = grad_attended.reshape(items, local, HEADS, HDIM)
        soft = jnp.exp(self.scores() - self.log_total)
        grad_soft = jnp.einsum(
            "iqhd,kilhd->ihqkl", grad_attended, self.values, preferred_element_type=F32
        )
        mean = jnp.sum(soft * grad_soft, axis=(3, 4), keepdims=True)
        grad_scores = (soft * (grad_soft - mean)).astype(BF16)
        grad_queries = (
            jnp.einsum("ihqkl,kilhd->iqhd", grad_scores, self.keys, preferred_element_type=F32)
            * HDIM ** (-0.5)
        )
        grad_keys = (
            jnp.einsum("ihqkl,iqhd->kilhd", grad_scores, self.queries, preferred_element_type=F32)
            * HDIM ** (-0.5)
        )
        grad_values = jnp.einsum(
            "ihqkl,iqhd->kilhd", soft.astype(BF16), grad_attended, preferred_element_type=F32
        )
        shape = (self.hid, items, local, width)
        grad_kv = jnp.concatenate([grad_keys.reshape(shape), grad_values.reshape(shape)], axis=-1)
        own = lax.psum_scatter(grad_kv.astype(BF16), "hid", scatter_dimension=0, tiled=True)[0]
        rows = jnp.concatenate(
            [grad_queries.reshape(items, local, width).astype(BF16), own], axis=-1
        ).reshape(-1, 3 * width)
        grad_in = dot_t(rows, self.qkv).reshape(items, local, width)
        return grad_in, t_dot(self.hidden, rows), out_grad

    def join_qkv(self, parts):
        return jnp.sum(parts.astype(F32), axis=0).astype(BF16)


def spread_rows(grad):
    hid, dp = lax.axis_size("hid"), lax.axis_size("dp")
    rows, cols = grad.shape
    parts = grad.astype(BF16).reshape(hid, dp, rows // (hid * dp), cols).transpose(1, 0, 2, 3)
    summed = jnp.sum(exchange(parts, "dp").astype(F32), axis=0).astype(BF16)
    return exchange(summed, "hid")


def dp_sum(grad):
    dp = lax.axis_size("dp")
    rows, cols = grad.shape
    parts = exchange(grad.astype(BF16).reshape(dp, rows // dp, cols), "dp")
    return jnp.sum(parts.astype(F32), axis=0).astype(BF16)


def dp_join(rows):
    return lax.all_gather(rows, "dp", axis=0, tiled=True).astype(F32)


def shards(
    tokens,
    cotangent,
    item_lengths,
    time_steps,
    class_labels,
    routes,
    time_table,
    class_table,
    modulation,
    qkv_weight,
    out_weight,
    router,
    shared_up,
    shared_down,
    expert_up,
    expert_down,
):
    hid_count = lax.axis_size("hid")
    dp_count = lax.axis_size("dp")
    hid_rank = lax.axis_index("hid")
    dp_rank = lax.axis_index("dp")
    item_count, local_len, width = tokens.shape
    full_len = routes.shape[1]
    top_count = routes.shape[2]
    capacity = item_count * full_len * top_count * 5 // (4 * dp_count)
    row_count = item_count * local_len
    group_rows = hid_count * row_count
    slot_rows = dp_count * capacity
    own_width = modulation.shape[0]

    split = HeadSplit if HEADS % hid_count == 0 else PatchSplit
    attention = split(tokens, qkv_weight, out_weight, item_lengths)
    cot_all = lax.all_gather(cotangent[None], "hid", axis=0, tiled=True)

    def owned_rows(table, index):
        rows = table.shape[0]
        local = index - hid_rank * rows
        picked = jnp.take(table, jnp.clip(local, 0, rows - 1), axis=0).astype(F32)
        return jnp.where(((local >= 0) & (local < rows))[:, None], picked, 0.0)

    cond = small_sum(
        owned_rows(time_table, time_steps) + owned_rows(class_table, class_labels), "hid"
    )
    scaled = jax.nn.silu(cond).astype(BF16)
    scaled_own = lax.dynamic_slice_in_dim(scaled, hid_rank * own_width, own_width, 1)
    router_slot = lax.dynamic_update_slice_in_dim(
        jnp.zeros((dp_count, width), F32), router.T.astype(F32), hid_rank * own_width, 1
    )
    early = small_sum(
        jnp.concatenate([dot(scaled_own, modulation), router_slot.reshape(1, -1)], axis=1)
        if item_count == 1
        else jnp.concatenate(
            [dot(scaled_own, modulation).reshape(1, -1), router_slot.reshape(1, -1)], axis=1
        ),
        "hid",
    )
    shift_size = item_count * 6 * width
    shifts = early[:, :shift_size].reshape(item_count, 6, 1, width)
    router_rows = early[:, shift_size:].reshape(dp_count, width).astype(BF16)
    shift_in = shifts[:, 0]
    scale_in = shifts[:, 1]
    gate_in = shifts[:, 2]
    shift_mid = shifts[:, 3]
    scale_mid = shifts[:, 4]
    gate_mid = shifts[:, 5]

    group_routes = (
        routes.reshape(item_count, hid_count, local_len, top_count)
        .transpose(1, 0, 2, 3)
        .reshape(group_rows, top_count)
    )
    pair_routes = group_routes.reshape(-1)
    expert_hot = (pair_routes[:, None] == jnp.arange(dp_count, dtype=jnp.int32)[None, :]).astype(
        jnp.int32
    )
    slot_of = jnp.sum(jnp.cumsum(expert_hot, axis=0) * expert_hot, axis=1) - 1
    target = pair_routes * capacity + slot_of
    pair_count = group_rows * top_count
    pair_of = (
        jnp.full((slot_rows,), pair_count, jnp.int32)
        .at[target]
        .set(jnp.arange(pair_count, dtype=jnp.int32), unique_indices=True, mode="promise_in_bounds")
    )
    token_of = pair_of // top_count
    swapped = jnp.concatenate([group_routes[:, ::-1].reshape(-1), jnp.zeros((1,), jnp.int32)])
    other_out = swapped.at[pair_of].get(mode="promise_in_bounds").reshape(dp_count, 1, capacity)
    other = exchange(other_out, "dp").reshape(slot_rows, 1)
    target_pairs = target.reshape(group_rows, top_count)

    grad_rows = (gate_mid[None] * cot_all.astype(F32)).astype(BF16).reshape(group_rows, width)
    grads_pad = jnp.concatenate([grad_rows, jnp.zeros((8, width), BF16)], axis=0)
    send_grads = grads_pad.at[token_of].get(mode="promise_in_bounds")
    expert_grads = exchange(send_grads.reshape(dp_count, capacity, width), "dp").reshape(
        slot_rows, width
    )

    tokens_f = tokens.astype(F32)
    normed_in, inverse_in = layer_norm(tokens_f)
    branch = attention.forward(shift_in, scale_in).reshape(item_count, local_len, width)
    residual = tokens_f + gate_in * branch
    normed_mid, inverse_mid = layer_norm(residual)
    hidden_mid = (normed_mid * (1.0 + scale_mid) + shift_mid).astype(BF16)
    mid_rows = lax.all_gather(hidden_mid[None], "hid", axis=0, tiled=True).reshape(
        group_rows, width
    )
    send_rows = mid_rows.at[jnp.minimum(token_of, group_rows - 1)].get(mode="promise_in_bounds")
    expert_rows = exchange(send_rows.reshape(dp_count, capacity, width), "dp").reshape(
        slot_rows, width
    )

    shared_gelu, shared_slope = gelu_pair(dot(mid_rows, shared_up))
    shared_act = shared_gelu.astype(BF16)
    grad_shared_pre = (dot_t(grad_rows, shared_down) * shared_slope).astype(BF16)
    grad_mid_part = dot_t(grad_shared_pre, shared_up)
    shared_out = dot(shared_act, shared_down)

    up, down = expert_up[0], expert_down[0]
    logits = dot_t(expert_rows, router_rows)
    ranks = jnp.arange(dp_count, dtype=jnp.int32)[None, :]
    own_hot = (ranks == dp_rank).astype(F32)
    other_hot = (ranks == other).astype(F32)
    gap = jnp.sum(logits * (other_hot - own_hot), axis=1, keepdims=True)
    gate_full = 1.0 / (1.0 + jnp.exp(gap))
    gate_rest = 1.0 / (1.0 + jnp.exp(-gap))
    gate = gate_full.astype(BF16).astype(F32)
    expert_gelu, expert_slope = gelu_pair(dot(expert_rows, up))
    grad_expert_act = dot_t(expert_grads, down)
    grad_gate = jnp.sum(grad_expert_act * expert_gelu, axis=1, keepdims=True)
    grad_expert_pre = (grad_expert_act * gate * expert_slope).astype(BF16)
    grad_logits = (gate_full * gate_rest * grad_gate) * (own_hot - other_hot)
    logits_high = grad_logits.astype(BF16)
    logits_low = (grad_logits - logits_high.astype(F32)).astype(BF16)
    slot_grads = (
        dot_t(grad_expert_pre, up) + dot(logits_high, router_rows) + dot(logits_low, router_rows)
    ).astype(BF16)
    back_rows = exchange(slot_grads.reshape(dp_count, capacity, width), "dp").reshape(
        slot_rows, width
    )
    expert_act = (gate * expert_gelu).astype(BF16)
    expert_out = dot(expert_act, down).astype(BF16)
    returned = exchange(expert_out.reshape(dp_count, capacity, width), "dp").reshape(
        slot_rows, width
    )
    router_part = t_dot(logits_high, expert_rows) + t_dot(logits_low, expert_rows)
    expert_down_grad = t_dot(expert_act, expert_grads)[None]
    expert_up_grad = t_dot(expert_rows, grad_expert_pre)[None]
    shared_down_rows = dp_sum(t_dot(shared_act, grad_rows))
    shared_up_rows = dp_sum(t_dot(mid_rows, grad_shared_pre))

    def combine(rows, start):
        total = start
        for j in range(top_count):
            total = total + rows.at[target_pairs[:, j]].get(mode="promise_in_bounds").astype(F32)
        return lax.psum_scatter(
            total.astype(BF16).reshape(hid_count, item_count, local_len, width),
            "hid",
            scatter_dimension=0,
            tiled=True,
        )[0].astype(F32)

    grad_mid = combine(back_rows, grad_mid_part)
    grad_out = cotangent.astype(F32)
    grad_scale_mid = jnp.sum(grad_mid * normed_mid, axis=1)
    grad_shift_mid = jnp.sum(grad_mid, axis=1)
    grad_residual = grad_out + norm_back(grad_mid * (1.0 + scale_mid), normed_mid, inverse_mid)
    grad_gate_in = jnp.sum(grad_residual * branch, axis=1)
    grad_branch = (gate_in * grad_residual).astype(BF16).reshape(row_count, width)

    moe = combine(returned, shared_out)
    output = (residual + gate_mid * moe).astype(BF16)
    grad_gate_mid = jnp.sum(grad_out * moe, axis=1)

    grad_in, qkv_grad, out_grad = attention.backward(grad_branch)
    grad_scale_in = jnp.sum(grad_in * normed_in, axis=1)
    grad_shift_in = jnp.sum(grad_in, axis=1)
    tokens_grad = grad_residual + norm_back(grad_in * (1.0 + scale_in), normed_in, inverse_in)

    grad_shifts = jnp.stack(
        [grad_shift_in, grad_scale_in, grad_gate_in, grad_shift_mid, grad_scale_mid, grad_gate_mid],
        axis=1,
    ).reshape(item_count, 6 * width)
    shifts_all = lax.all_gather(small_sum(grad_shifts, "hid"), "dp", axis=0, tiled=True)
    marks = jnp.stack([time_steps, class_labels], axis=1).astype(F32)
    notes = lax.all_gather(jnp.concatenate([cond, marks], axis=1), "dp", axis=0, tiled=True)
    cond_own = lax.dynamic_slice_in_dim(notes[:, :width], hid_rank * own_width, own_width, 1)
    scaled_all = jax.nn.silu(cond_own).astype(BF16).astype(F32)
    modulation_grad = exact_dot(scaled_all.T, shifts_all)
    grad_cond_own = silu_back(cond_own, exact_dot(shifts_all, modulation.astype(F32).T))
    grad_cond = copies(grad_cond_own, "hid").transpose(1, 0, 2).reshape(-1, width)

    def table_grad(table, index):
        rows = table.shape[0]
        positions = (hid_rank * rows + jnp.arange(rows, dtype=jnp.int32)).astype(F32)
        return exact_dot((positions[:, None] == index[None, :]).astype(F32), grad_cond)

    time_grad = table_grad(time_table, notes[:, width])
    class_grad = table_grad(class_table, notes[:, width + 1])

    router_sum = small_sum(small_sum(router_part, "hid"), "dp")
    router_grad = lax.dynamic_slice_in_dim(router_sum, hid_rank * own_width, own_width, 1).T

    out_rows = jnp.sum(spread_rows(out_grad).astype(F32), axis=0).astype(BF16)
    qkv_rows = attention.join_qkv(spread_rows(qkv_grad))
    return (
        output,
        tokens_grad,
        time_grad,
        class_grad,
        modulation_grad,
        dp_join(qkv_rows),
        dp_join(out_rows),
        router_grad,
        dp_join(shared_up_rows),
        dp_join(shared_down_rows),
        expert_up_grad,
        expert_down_grad,
    )


def solution(mesh):
    placed = (
        P("dp", "hid", None),
        P("dp", "hid", None),
        P("dp"),
        P("dp"),
        P("dp"),
        P("dp", None, None),
        P("hid", None),
        P("hid", None),
        P("hid", None),
        P("hid", None),
        P("hid", None),
        P("hid", None),
        P(None, "hid"),
        P("hid", None),
        P("dp", None, "hid"),
        P("dp", "hid", None),
    )
    return jax.shard_map(
        shards,
        mesh=mesh,
        in_specs=placed,
        out_specs=(
            P("dp", "hid", None),
            P("dp", "hid", None),
            P("hid", None),
            P("hid", None),
            P("hid", None),
            P("hid", None),
            P("hid", None),
            P("hid", None),
            P(None, "hid"),
            P("hid", None),
            P("dp", None, "hid"),
            P("dp", "hid", None),
        ),
        check_vma=False,
    )
```

time: 1380 us -> 672 us (0.49)
  waiting for transfers between devices: 736 us -> 206 us
  blocking collectives: 201 us -> 67.7 us
  other arithmetic: 99.9 us -> 43.2 us
  local copies, waits for them, and re-layouts: 149 us -> 103 us
  starting transfers between devices: 35.3 us -> 80.5 us
  Pallas kernels: 0 us -> 27.8 us
  matrix products: 136 us -> 117 us
    all_gather x7 -> x5, waiting for transfers between devices: 317 us -> 56.6 us  [the longest x1 37.8 us: shards(): cot_all = lax.all_gather(cotangent[None], 'hid', axis=0, tiled=True)]
    reduce_scatter x6 -> x3, waiting for transfers between devices: 175 us -> 0.02 us  [the longest x2 0.02 us: combine(): lax.psum_scatter(total.astype(BF16).reshape(hid_count, item_count, local_...]
    unnamed x2 -> x0, blocking collectives: 115 us -> none
    psum x1 -> x0, waiting for transfers between devices: 91.2 us -> none  [shards(): lax.psum(time_shard.astype(jnp.bfloat16), 'dp').astype(jnp.float32)]
    all_to_all x5 -> x19, starting transfers between devices: 21.4 us -> 79.7 us  [exchange(): return lax.all_to_all(values, axis, split_axis=0, concat_axis=0, tiled=True)]
    all_to_all x1, blocking collectives: 50.7 us -> 20.3 us  [exchange(): return lax.all_to_all(values, axis, split_axis=0, concat_axis=0, tiled=True)]
    pallas_call x0 -> x2, Pallas kernels: none -> 27.8 us  [the longest x1 14.8 us: attend_back(): pl.pallas_call(functools.partial(attend_back_kernel, heads=heads), grid_s...]
    all_gather x2 -> x4, blocking collectives: 22.8 us -> 47.4 us  [the longest x1 19.9 us: shards(): lax.all_gather(jnp.concatenate([cond, marks], axis=1), 'dp', axis=0, tile...]
  transfers between devices with their start and end apart: 23 -> 28, of which waited for: 16 -> 16; matrix products, arithmetic and copies ran while one was open for 27% -> 35% of each run, Pallas kernels for 0% -> 4%
where the time goes in v1:
time: 672 us; the launch traced here: 663 us
  waiting for transfers between devices  206 us (31%)
  matrix products  117 us (17%)
  local copies, waits for them, and re-layouts  103 us (15%)
  starting transfers between devices  80.5 us (12%)
  blocking collectives  67.7 us (10%)
  other arithmetic  43.2 us (6%)
  Pallas kernels  27.8 us (4%)
  between operations  17.1 us (3%)
    all_to_all x19, waiting for transfers between devices, exchange(): return lax.all_to_all(values, axis, split_axis=0, concat_axis=0, tiled=True)  142 us
    all_to_all x19, starting transfers between devices, exchange(): return lax.all_to_all(values, axis, split_axis=0, concat_axis=0, tiled=True)  79.7 us
    dot_general x9, matrix products, dot(): return jnp.dot(left, right, preferred_element_type=F32)  41 us
    all_gather x1, waiting for transfers between devices, shards(): cot_all = lax.all_gather(cotangent[None], 'hid', axis=0, tiled=True)  37.8 us
    dot_general x8, matrix products, t_dot(): lax.dot_general(left, right, (((0,), (0,)), ((), ())), preferred_element_...  34.9 us
    dot_general x7, matrix products, dot_t(): lax.dot_general(left, right, (((1,), (1,)), ((), ())), preferred_element_...  33.4 us
    gather x4, local copies, waits for them, and re-layouts, combine(): rows.at[target_pairs[:, j]].get(mode='promise_in_bounds').astype(F32)  32.8 us
    all_to_all x1, blocking collectives, exchange(): return lax.all_to_all(values, axis, split_axis=0, concat_axis=0, tiled=True)  20.3 us
  transfers between devices with their start and end apart: 28, of which 16 were waited for; matrix products, arithmetic and copies ran while one was open for 35% of the time, Pallas kernels for 4%

profile of v1, /device:TPU:0, one launch (start us, length us, event | category | flops | bytes accessed | tf_op | source)
XLA Modules:
  0.0 662.7 jit_solution(7872352367776312083)
XLA Ops:
  10.7 6.3 all-to-all-start
  18.0 4.7 all-to-all-done
  34.7 4.5 all-to-all-done.1
  39.2 4.2 all-to-all-start.2
  43.8 18.7 %all-gather.19.cloned.1.call-done = bf16[4,256,768]{2,1,0:T(8,128)(2,1)} async-done(((bf16[1,256,768]{2,1,0:T(8,128)(2,1)}), bf16[4,256,768]{2,1,0:T(8,128)(2,1)}) %all-gather.19.cloned.1.call-update) | async-done | bytes 1572880 | tf_op jit(solution)/shard_map/all_gather | solution.py:202
  68.3 5.9 all-to-all-done.2
  78.3 13.0 %attend.1 = (bf16[1,1024,192]{2,1,0:T(8,128)(2,1)}, f32[1,8,1024]{2,1,0:T(8,128)}) custom-call(s32[1]{0:T(128)S(6)} %copy.131.length_ref, bf16[1,1024,576]{2,1,0:T(8,128)(2,1)} %fusion.8.query_ref.all_ref, bf16[1,1024,576]{2,1,0:T(8,128)(2,1)} %fusion.8.query_ref.all_ref), custom_call_target="tpu_custom_call" | custom-call | tf_op jit(solution)/shard_map/attend/pallas_call | solution.py:141
  97.3 11.1 %all-to-all-done.3 = bf16[4,1,256,192]{2,3,1,0:T(8,128)(2,1)S(1)} async-done(((bf16[4,1,256,192]{2,3,1,0:T(8,128)(2,1)}), bf16[4,1,256,192]{2,3,1,0:T(8,128)(2,1)S(1)}, u32[]{:S(2)}, u32[]{:S(2)}) %all-to-all-start.3) | async-done | bytes 393248 | tf_op jit(solution)/shard_map/all_to_all | solution.py:60
  118.9 8.1 %scatter_custom_fusion = s32[2560]{0:T(1024)S(1)} fusion(s32[2048]{0:T(1024)S(1)} %bitcast.267, s32[2048]{0:T(1024)S(1)} %iota.22, s32[]{:T(128)} %constant.109.clone.1), kind=kCustom, calls=%fused_computation.174 | custom fusion | bytes 10244 | tf_op jit(solution)/shard_map/scatter | solution.py:428
  127.1 13.6 %gather_fusion.1 = s32[2560]{0:T(1024)S(1)} fusion(s32[2049]{0:T(1024)S(1)} %pad_add_fusion, s32[3072]{0:T(1024)S(1)} %get-tuple-element.60), kind=kCustom, calls=%fused_computation.1 | custom fusion | bytes 30720 | tf_op jit(solution)/shard_map/gather | solution.py:432
  145.0 4.9 all-gather.21.cloned.1.call-done
  149.9 11.9 %gather_fusion = bf16[2560,768]{1,0:T(8,128)(2,1)} fusion(bf16[1024,768]{1,0:T(8,128)(2,1)} %bitcast.230, s32[3072]{0:T(1024)S(1)} %pad_clamp_fusion.2), kind=kCustom, calls=%fused_computation | custom fusion | bytes 7874560 | tf_op jit(solution)/shard_map/gather | solution.py:452
  161.8 4.5 all-to-all-start.4
  166.9 37.8 %all-gather.23.cloned.1.call-done = bf16[4,256,768]{2,1,0:T(8,128)(2,1)} async-done(((bf16[1,256,768]{2,1,0:T(8,128)(2,1)}), bf16[4,256,768]{2,1,0:T(8,128)(2,1)}) %all-gather.23.cloned.1.call-update) | async-done | bytes 1572880 | tf_op jit(solution)/shard_map/all_gather | solution.py:379
  207.7 8.6 %gather_fusion.4 = bf16[2560,768]{1,0:T(8,128)(2,1)} fusion(bf16[1032,768]{1,0:T(8,128)(2,1)S(1)} %concatenate.22, s32[3072]{0:T(1024)S(1)} %get-tuple-element.59), kind=kCustom, calls=%fused_computation.4 | custom fusion | bytes 7874560 | tf_op jit(solution)/shard_map/gather | solution.py:438
  216.2 4.8 all-to-all-start.7
  224.7 7.6 %fusion.16 = f32[2560,768]{0,1:T(8,128)} fusion(bf16[2560,768]{1,0:T(8,128)(2,1)} %bitcast.25, bf16[1,768,768]{2,1,0:T(8,128)(2,1)S(1)} %copy-done.32), kind=kOutput, calls=%fused_computation.58 | convolution fusion | flops 3019898880 | bytes 12976128 | tf_op jit(solution)/shard_map/dot_general | solution.py:48
  232.2 35.1 %all-to-all-done.7 = bf16[8,320,768]{2,1,0:T(8,128)(2,1)} async-done(((bf16[8,320,768]{2,1,0:T(8,128)(2,1)}), bf16[8,320,768]{2,1,0:T(8,128)(2,1)}, u32[]{:S(2)}, u32[]{:S(2)}) %all-to-all-start.7) | async-done | bytes 3932192 | tf_op jit(solution)/shard_map/all_to_all | solution.py:60
  267.3 10.4 %multiply_reduce_fusion = (f32[2560]{0:T(1024)S(1)}, bf16[2560,768]{0,1:T(8,128)(2,1)S(1)}) fusion(f32[2560,768]{0,1:T(8,128)} %fusion.16, f32[2560]{0:T(1024)S(1)} %fusion.92, bf16[2560,768]{1,0:T(8,128)(2,1)} %bitcast.36, bf16[1,768,768]{2,1,0:T(8,128)(2,1)} %param.33), kind=kOutput, calls=%fused_computation.9 | convolution fusion | flops 3063150080 | bytes 16928768 | tf_op jit(solution)/shard_map/dot_general | solution.py:52
  285.6 5.0 all-to-all-start.8
  293.7 4.4 fusion.113
  298.2 10.1 %convolution_convert_fusion = bf16[2560,768]{1,0:T(8,128)(2,1)} fusion(bf16[1,768,768]{2,1,0:T(8,128)(2,1)S(1)} %copy-done.33, f32[2560]{0:T(1024)S(1)} %fusion.92, f32[2560,768]{0,1:T(8,128)} %fusion.16), kind=kOutput, calls=%fused_computation.16 | convolution fusion | flops 3041525760 | bytes 12986368 | tf_op jit(solution)/shard_map/dot_general | solution.py:48
  308.2 28.7 %all-to-all-done.8 = bf16[8,320,768]{2,1,0:T(8,128)(2,1)} async-done(((bf16[8,320,768]{2,1,0:T(8,128)(2,1)}), bf16[8,320,768]{2,1,0:T(8,128)(2,1)}, u32[]{:S(2)}, u32[]{:S(2)}) %all-to-all-start.8) | async-done | bytes 3932192 | tf_op jit(solution)/shard_map/all_to_all | solution.py:60
  337.0 4.5 all-to-all-start.6
  341.7 6.4 multiply_convert_fusion.2
  348.1 8.2 %gather_fusion.6 = bf16[1024,768]{1,0:T(8,128)(2,1)} fusion(bf16[2560,768]{1,0:T(8,128)(2,1)} %bitcast.38, s32[1024]{0:T(1024)S(1)} %get-tuple-element.61), kind=kCustom, calls=%fused_computation.6 | custom fusion | bytes 3149824 | tf_op jit(solution)/shard_map/gather | solution.py:499
  356.3 8.2 %gather_fusion.5 = bf16[1024,768]{1,0:T(8,128)(2,1)} fusion(bf16[2560,768]{1,0:T(8,128)(2,1)} %bitcast.38, s32[1024]{0:T(1024)S(1)} %get-tuple-element.62), kind=kCustom, calls=%fused_computation.5 | custom fusion | bytes 3149824 | tf_op jit(solution)/shard_map/gather | solution.py:499
  364.5 5.3 add_convert_fusion.1
  369.9 17.9 %all-to-all-done.6 = bf16[8,320,768]{2,1,0:T(8,128)(2,1)} async-done(((bf16[8,320,768]{2,1,0:T(8,128)(2,1)}), bf16[8,320,768]{2,1,0:T(8,128)(2,1)}, u32[]{:S(2)}, u32[]{:S(2)}) %all-to-all-start.6) | async-done | bytes 3932192 | tf_op jit(solution)/shard_map/all_to_all | solution.py:60
  387.8 8.2 %gather_fusion.3 = bf16[1024,768]{1,0:T(8,128)(2,1)} fusion(bf16[2560,768]{1,0:T(8,128)(2,1)} %bitcast.30, s32[1024]{0:T(1024)S(1)} %get-tuple-element.61), kind=kCustom, calls=%fused_computation.3 | custom fusion | bytes 3149824 | tf_op jit(solution)/shard_map/gather | solution.py:499
  396.0 8.2 %gather_fusion.2 = bf16[1024,768]{1,0:T(8,128)(2,1)} fusion(bf16[2560,768]{1,0:T(8,128)(2,1)} %bitcast.30, s32[1024]{0:T(1024)S(1)} %get-tuple-element.62), kind=kCustom, calls=%fused_computation.2 | custom fusion | bytes 3149824 | tf_op jit(solution)/shard_map/gather | solution.py:499
  404.2 6.5 add_convert_fusion.2
  410.7 4.2 convolution_convert_fusion.3
  414.9 20.3 %all_to_all.100 = bf16[8,96,768]{2,1,0:T(8,128)(2,1)} all-to-all(bf16[8,96,768]{2,1,0:T(8,128)(2,1)S(1)} %bitcast.256), channel_id=1, replica_groups=mesh['dp'=8,'hid'=4] {'dp'}, dimensions={0} | all-to-all | bytes 2359296 | tf_op jit(solution)/shard_map/all_to_all | solution.py:60
  441.2 4.3 all-to-all-start.18
  451.1 12.8 %all-to-all-done.18 = bf16[8,96,768]{2,1,0:T(8,128)(2,1)} async-done(((bf16[8,96,768]{2,1,0:T(8,128)(2,1)}), bf16[8,96,768]{2,1,0:T(8,128)(2,1)}, u32[]{:S(2)}, u32[]{:S(2)}) %all-to-all-start.18) | async-done | bytes 1179680 | tf_op jit(solution)/shard_map/all_to_all | solution.py:60
  491.0 10.8 %all-to-all-done.9 = bf16[4,1,256,192]{2,3,1,0:T(8,128)(2,1)S(1)} async-done(((bf16[4,1,256,192]{2,3,1,0:T(8,128)(2,1)}), bf16[4,1,256,192]{2,3,1,0:T(8,128)(2,1)S(1)}, u32[]{:S(2)}, u32[]{:S(2)}) %all-to-all-start.9) | async-done | bytes 393248 | tf_op jit(solution)/shard_map/all_to_all | solution.py:60
  501.7 4.2 all-to-all-start.14
  506.1 19.9 %all-gather.4 = f32[8,1,770]{2,1,0:T(1,128)S(1)} all-gather(f32[1,1,770]{2,1,0:T(1,128)S(1)} %maximum_bitcast_fusion), channel_id=1, replica_groups=mesh['dp'=8,'hid'=4] {'dp'}, dimensions={0}, use_global_device_ids=true | all-gather | bytes 27720 | tf_op jit(solution)/shard_map/all_gather | solution.py:530
  527.0 14.8 %attend_back.1 = bf16[1,1024,576]{2,1,0:T(8,128)(2,1)} custom-call(s32[1]{0:T(128)S(6)} %copy.131.length_ref, bf16[1,1024,576]{2,1,0:T(8,128)(2,1)} %fusion.8.query_ref.all_ref, bf16[1,1024,192]{2,1,0:T(8,128)(2,1)} %bitcast.248, bf16[1,1024,576]{2,1,0:T(8,128)(2,1)} %fusion.8.query_ref.all_ref, f32[1,8,1024]{2,1,0:T(8,128)} %get-tuple-element.16.log_ref), custom_call_target="tpu_custom_call" | custom-call | tf_op jit(solution)/shard_map/attend_back/pallas_call | solution.py:168
  559.2 4.2 all-to-all-start.12
  563.4 10.7 %convolution_bitcast_fusion = f32[1,768,768]{2,1,0:T(8,128)} fusion(bf16[2560,768]{1,0:T(8,128)(2,1)} %bitcast.36, f32[2560]{0:T(1024)S(1)} %copy-done.29, f32[2560,768]{0,1:T(8,128)} %fusion.16), kind=kOutput, calls=%fused_computation.36 | convolution fusion | flops 3039559680 | bytes 14166016 | tf_op jit(solution)/shard_map/dot_general | solution.py:56
  581.7 8.0 %convolution_bitcast_fusion.1 = f32[1,768,768]{2,1,0:T(8,128)} fusion(bf16[2560,768]{1,0:T(8,128)(2,1)} %bitcast.25, bf16[2560,768]{0,1:T(8,128)(2,1)} %copy-done.34), kind=kOutput, calls=%fused_computation.37 | convolution fusion | flops 3019898880 | bytes 10223616 | tf_op jit(solution)/shard_map/dot_general | solution.py:56
  592.4 5.1 all-to-all-start.13
  597.7 8.6 %all_gather.37 = bf16[192,768]{1,0:T(8,128)(2,1)S(1)} all-gather(bf16[24,768]{1,0:T(8,128)(2,1)S(1)} %reduce_sum.309), channel_id=1, replica_groups=mesh['dp'=8,'hid'=4] {'dp'}, dimensions={0}, use_global_device_ids=true | all-gather | bytes 331776 | tf_op jit(solution)/shard_map/all_gather | solution.py:343
  607.6 10.6 %all_gather.36 = bf16[192,2304]{1,0:T(8,128)(2,1)S(1)} all-gather(bf16[24,2304]{1,0:T(8,128)(2,1)S(1)} %reshape.873), channel_id=1, replica_groups=mesh['dp'=8,'hid'=4] {'dp'}, dimensions={0}, use_global_device_ids=true | all-gather | bytes 995328 | tf_op jit(solution)/shard_map/all_gather | solution.py:343
  622.9 5.1 all-to-all-start.10
  633.8 8.3 %all-gather.5 = f32[8,1,4608]{2,1,0:T(1,128)S(1)} all-gather(f32[1,1,4608]{2,1,0:T(1,128)S(1)} %reshape.992), channel_id=5, replica_groups=mesh['dp'=8,'hid'=4] {'dp'}, dimensions={0}, use_global_device_ids=true | all-gather | bytes 165888 | tf_op jit(solution)/shard_map/all_gather | solution.py:528
  (251 shorter events, 156.7 us)
Async XLA Ops:
  7.2 15.5 %copy-start = (bf16[192,4608]{1,0:T(8,128)(2,1)S(1)}, bf16[192,4608]{1,0:T(8,128)(2,1)}, u32[]{:S(2)}) copy-start(bf16[192,4608]{1,0:T(8,128)(2,1)} %param.26) | copy-start | bytes 5308420
  7.2 21.5 %copy-start.15 = (bf16[192,2304]{1,0:T(8,128)(2,1)S(1)}, bf16[192,2304]{1,0:T(8,128)(2,1)}, u32[]{:S(2)}) copy-start(bf16[192,2304]{1,0:T(8,128)(2,1)} %param.27) | copy-start | bytes 2654212
  7.2 55.3 %all-gather.19.cloned.1.call-start = ((), (), s32[]{:S(2)}) async-start(), calls=%async_computation.29 | async-start | bytes 1966080 | tf_op jit(solution)/shard_map/all_gather | solution.py:202
  10.7 11.9 %all-to-all-start = ((f32[4,1,768]{2,1,0:T(1,128)}), f32[4,1,768]{2,1,0:T(1,128)S(1)}, u32[]{:S(2)}, u32[]{:S(2)}) async-start(f32[4,1,768]{2,1,0:T(1,128)} %broadcast_in_dim.132), calls=%async_computation | async-start | bytes 24576 | tf_op jit(solution)/shard_map/all_to_all | solution.py:60
  22.7 6.1 copy-start.19
  24.0 15.2 %all-to-all-start.1 = ((f32[4,1,10752]{2,1,0:T(1,128)}), f32[4,1,10752]{2,1,0:T(1,128)S(1)}, u32[]{:S(2)}, u32[]{:S(2)}) async-start(f32[4,1,10752]{2,1,0:T(1,128)} %broadcast_in_dim.135), calls=%async_computation.1 | async-start | bytes 344064 | tf_op jit(solution)/shard_map/all_to_all | solution.py:60
  27.3 70.0 %all-gather.13.cloned.1.call-start = ((), (), s32[]{:S(2)}) async-start(), calls=%async_computation.23 | async-start | bytes 1474560 | tf_op jit(solution)/shard_map/all_gather | solution.py:201
  39.2 35.0 %all-to-all-start.2 = ((bf16[4,192,576]{2,1,0:T(8,128)(2,1)}), bf16[4,192,576]{2,1,0:T(8,128)(2,1)}, u32[]{:S(2)}, u32[]{:S(2)}) async-start(bf16[4,192,576]{2,1,0:T(8,128)(2,1)} %copy.89), calls=%async_computation.2 | async-start | bytes 1966080 | tf_op jit(solution)/shard_map/all_to_all | solution.py:60
  43.8 22.8 %copy-start.16 = (f32[768]{0:T(1024)}, f32[768]{0:T(1024)S(1)}, u32[]{:S(2)}) copy-start(f32[768]{0:T(1024)S(1)} %get-tuple-element.42) | copy-start | bytes 9220
  78.3 18.8 %copy-start.6 = (bf16[1,256,768]{2,1,0:T(8,128)(2,1)S(1)}, bf16[1,256,768]{2,1,0:T(8,128)(2,1)}, u32[]{:S(2)}) copy-start(bf16[1,256,768]{2,1,0:T(8,128)(2,1)} %param.18) | copy-start | bytes 1179652
  93.4 15.0 %all-to-all-start.3 = ((bf16[4,1,256,192]{2,3,1,0:T(8,128)(2,1)}), bf16[4,1,256,192]{2,3,1,0:T(8,128)(2,1)S(1)}, u32[]{:S(2)}, u32[]{:S(2)}) async-start(bf16[4,1,256,192]{2,3,1,0:T(8,128)(2,1)} %copy.91), calls=%async_computation.3 | async-start | bytes 786432 | tf_op jit(solution)/shard_map/all_to_all | solution.py:60
  96.8 16.8 %copy-start.18 = (s32[1,1024,2]{1,2,0:T(2,128)S(1)}, s32[1,1024,2]{1,2,0:T(2,128)}, u32[]{:S(2)}) copy-start(s32[1,1024,2]{1,2,0:T(2,128)} %param.23) | copy-start | bytes 24580
  96.8 53.0 %all-gather.21.cloned.1.call-start = ((), (), s32[]{:S(2)}) async-start(), calls=%async_computation.30 | async-start | bytes 1966080 | tf_op jit(solution)/shard_map/all_gather | solution.py:449
  97.3 16.6 %copy-start.21 = (f32[256]{0:T(256)}, f32[256]{0:T(256)S(1)}, u32[]{:S(2)}) copy-start(f32[256]{0:T(256)S(1)} %broadcast_multiply_fusion.4) | copy-start | bytes 3076
  141.4 20.4 %all-to-all-start.5 = ((s32[8,1,320]{2,1,0:T(1,128)}), s32[8,1,320]{2,1,0:T(1,128)S(1)}, u32[]{:S(2)}, u32[]{:S(2)}) async-start(s32[8,1,320]{2,1,0:T(1,128)} %reshape.857), calls=%async_computation.5 | async-start | bytes 24576 | tf_op jit(solution)/shard_map/all_to_all | solution.py:60
  161.8 54.5 %all-to-all-start.4 = ((bf16[8,320,768]{2,1,0:T(8,128)(2,1)}), bf16[8,320,768]{2,1,0:T(8,128)(2,1)}, u32[]{:S(2)}, u32[]{:S(2)}) async-start(bf16[8,320,768]{2,1,0:T(8,128)(2,1)} %bitcast.235), calls=%async_computation.4 | async-start | bytes 7864320 | tf_op jit(solution)/shard_map/all_to_all | solution.py:60
  166.3 38.4 %all-gather.23.cloned.1.call-start = ((), (), s32[]{:S(2)}) async-start(), calls=%async_computation.31 | async-start | bytes 1966080 | tf_op jit(solution)/shard_map/all_gather | solution.py:379
  216.2 51.1 %all-to-all-start.7 = ((bf16[8,320,768]{2,1,0:T(8,128)(2,1)}), bf16[8,320,768]{2,1,0:T(8,128)(2,1)}, u32[]{:S(2)}, u32[]{:S(2)}) async-start(bf16[8,320,768]{2,1,0:T(8,128)(2,1)} %bitcast.234), calls=%async_computation.8 | async-start | bytes 7864320 | tf_op jit(solution)/shard_map/all_to_all | solution.py:60
  224.7 73.5 %copy-start.28 = (f32[2560]{0:T(1024)}, f32[2560]{0:T(1024)S(1)}, u32[]{:S(2)}) copy-start(f32[2560]{0:T(1024)S(1)} %fusion.92) | copy-start | bytes 30724
  285.6 51.3 %all-to-all-start.8 = ((bf16[8,320,768]{2,1,0:T(8,128)(2,1)}), bf16[8,320,768]{2,1,0:T(8,128)(2,1)}, u32[]{:S(2)}, u32[]{:S(2)}) async-start(bf16[8,320,768]{2,1,0:T(8,128)(2,1)} %bitcast.233), calls=%async_computation.9 | async-start | bytes 7864320 | tf_op jit(solution)/shard_map/all_to_all | solution.py:60
  337.0 50.8 %all-to-all-start.6 = ((bf16[8,320,768]{2,1,0:T(8,128)(2,1)}), bf16[8,320,768]{2,1,0:T(8,128)(2,1)}, u32[]{:S(2)}, u32[]{:S(2)}) async-start(bf16[8,320,768]{2,1,0:T(8,128)(2,1)} %bitcast.245), calls=%async_computation.6 | async-start | bytes 7864320 | tf_op jit(solution)/shard_map/all_to_all | solution.py:60
  341.5 136.2 %reduce-scatter.6.cloned.1.call-start = ((), (), s32[]{:S(2)}) async-start(), calls=%async_computation.25 | async-start | bytes 1966080 | tf_op jit(solution)/shard_map/reduce_scatter | solution.py:500
  369.8 111.0 %reduce-scatter.4.cloned.1.call-start = ((), (), s32[]{:S(2)}) async-start(), calls=%async_computation.24 | async-start | bytes 1966080 | tf_op jit(solution)/shard_map/reduce_scatter | solution.py:500
  410.7 136.0 %all-gather.17.cloned.1.call-start = ((), (), s32[]{:S(2)}) async-start(), calls=%async_computation.28 | async-start | bytes 1327104 | tf_op jit(solution)/shard_map/all_gather | solution.py:343
  441.2 22.6 %all-to-all-start.18 = ((bf16[8,96,768]{2,1,0:T(8,128)(2,1)}), bf16[8,96,768]{2,1,0:T(8,128)(2,1)}, u32[]{:S(2)}, u32[]{:S(2)}) async-start(bf16[8,96,768]{2,1,0:T(8,128)(2,1)} %bitcast.255), calls=%async_computation.21 | async-start | bytes 2359296 | tf_op jit(solution)/shard_map/all_to_all | solution.py:60
  448.2 29.5 %copy-start.3 = (f32[1,256,768]{2,1,0:T(8,128)S(1)}, f32[1,256,768]{2,1,0:T(8,128)}, u32[]{:S(2)}) copy-start(f32[1,256,768]{2,1,0:T(8,128)} %copy-done.2) | copy-start | bytes 2359300
  448.2 29.5 %copy-start.24 = (f32[256]{0:T(256)S(1)}, f32[256]{0:T(256)}, u32[]{:S(2)}) copy-start(f32[256]{0:T(256)} %copy-done.23) | copy-start | bytes 3076
  464.5 9.1 %all-to-all-start.16 = ((f32[4,8,768]{2,1,0:T(8,128)}), f32[4,8,768]{2,1,0:T(8,128)S(1)}, u32[]{:S(2)}, u32[]{:S(2)}) async-start(f32[4,8,768]{2,1,0:T(8,128)} %broadcast_in_dim.146), calls=%async_computation.19 | async-start | bytes 196608 | tf_op jit(solution)/shard_map/all_to_all | solution.py:60
  467.8 81.8 %all-gather.15.cloned.1.call-start = ((), (), s32[]{:S(2)}) async-start(), calls=%async_computation.27 | async-start | bytes 1327104 | tf_op jit(solution)/shard_map/all_gather | solution.py:343
  474.3 11.5 %all-to-all-start.17 = ((f32[8,8,768]{2,1,0:T(8,128)}), f32[8,8,768]{2,1,0:T(8,128)S(1)}, u32[]{:S(2)}, u32[]{:S(2)}) async-start(f32[8,8,768]{2,1,0:T(8,128)} %broadcast_in_dim.147), calls=%async_computation.20 | async-start | bytes 393216 | tf_op jit(solution)/shard_map/all_to_all | solution.py:60
  485.8 15.9 %all-to-all-start.9 = ((bf16[4,1,256,192]{2,3,1,0:T(8,128)(2,1)}), bf16[4,1,256,192]{2,3,1,0:T(8,128)(2,1)S(1)}, u32[]{:S(2)}, u32[]{:S(2)}) async-start(bf16[4,1,256,192]{2,3,1,0:T(8,128)(2,1)} %bitcast.254), calls=%async_computation.11 | async-start | bytes 786432 | tf_op jit(solution)/shard_map/all_to_all | solution.py:60
  489.4 16.7 %copy-start.20 = (f32[1,768]{1,0:T(1,128)S(1)}, f32[1,768]{1,0:T(1,128)}, u32[]{:S(2)}) copy-start(f32[1,768]{1,0:T(1,128)} %copy-done.19) | copy-start | bytes 9220
  501.7 57.4 %all-to-all-start.14 = ((bf16[8,4,24,768]{3,2,1,0:T(8,128)(2,1)}), bf16[8,4,24,768]{3,2,1,0:T(8,128)(2,1)}, u32[]{:S(2)}, u32[]{:S(2)}) async-start(bf16[8,4,24,768]{3,2,1,0:T(8,128)(2,1)} %bitcast.241), calls=%async_computation.17 | async-start | bytes 2359296 | tf_op jit(solution)/shard_map/all_to_all | solution.py:60
  506.0 113.5 %reduce-scatter.8.cloned.1.call-start = ((), (), s32[]{:S(2)}) async-start(), calls=%async_computation.26 | async-start | bytes 1966080 | tf_op jit(solution)/shard_map/reduce_scatter | solution.py:240
  554.7 8.7 %copy-start.29 = (f32[2560]{0:T(1024)S(1)}, f32[2560]{0:T(1024)}, u32[]{:S(2)}) copy-start(f32[2560]{0:T(1024)} %copy-done.28) | copy-start | bytes 30724
  559.2 18.9 %all-to-all-start.12 = ((bf16[8,4,24,576]{3,2,1,0:T(8,128)(2,1)}), bf16[8,4,24,576]{3,2,1,0:T(8,128)(2,1)}, u32[]{:S(2)}, u32[]{:S(2)}) async-start(bf16[8,4,24,576]{3,2,1,0:T(8,128)(2,1)} %copy.103), calls=%async_computation.15 | async-start | bytes 1966080 | tf_op jit(solution)/shard_map/all_to_all | solution.py:60
  578.1 14.3 %all-to-all-start.15 = ((bf16[4,24,768]{2,1,0:T(8,128)(2,1)}), bf16[4,24,768]{2,1,0:T(8,128)(2,1)S(1)}, u32[]{:S(2)}, u32[]{:S(2)}) async-start(bf16[4,24,768]{2,1,0:T(8,128)(2,1)} %reduce_sum.308), calls=%async_computation.18 | async-start | bytes 294912 | tf_op jit(solution)/shard_map/all_to_all | solution.py:60
  581.6 15.8 %copy-start.10 = (bf16[1,1,256,768]{3,2,1,0:T(8,128)(2,1)S(1)}, bf16[1,1,256,768]{3,2,1,0:T(8,128)(2,1)}, u32[]{:S(2)}) copy-start(bf16[1,1,256,768]{3,2,1,0:T(8,128)(2,1)} %reduce-scatter.6.cloned.1.call-done) | copy-start | bytes 1179652
  581.6 15.9 %copy-start.25 = (f32[768]{0:T(1024)S(1)}, f32[768]{0:T(1024)}, u32[]{:S(2)}) copy-start(f32[768]{0:T(1024)} %get-tuple-element.28) | copy-start | bytes 9220
  581.6 15.9 %copy-start.27 = (f32[768]{0:T(1024)S(1)}, f32[768]{0:T(1024)}, u32[]{:S(2)}) copy-start(f32[768]{0:T(1024)} %get-tuple-element.44) | copy-start | bytes 9220
  581.6 15.9 %copy-start.26 = (f32[768]{0:T(1024)S(1)}, f32[768]{0:T(1024)}, u32[]{:S(2)}) copy-start(f32[768]{0:T(1024)} %get-tuple-element.51) | copy-start | bytes 9220
  592.4 14.7 %all-to-all-start.13 = ((bf16[4,24,576]{2,1,0:T(8,128)(2,1)}), bf16[4,24,576]{2,1,0:T(8,128)(2,1)S(1)}, u32[]{:S(2)}, u32[]{:S(2)}) async-start(bf16[4,24,576]{2,1,0:T(8,128)(2,1)} %reduce_sum.307), calls=%async_computation.16 | async-start | bytes 245760 | tf_op jit(solution)/shard_map/all_to_all | solution.py:60
  597.6 23.0 %copy-start.7 = (bf16[1,256,768]{2,1,0:T(8,128)(2,1)S(1)}, bf16[1,256,768]{2,1,0:T(8,128)(2,1)}, u32[]{:S(2)}) copy-start(bf16[1,256,768]{2,1,0:T(8,128)(2,1)} %param.18) | copy-start | bytes 1179652
  597.6 23.0 %copy-start.17 = (f32[768]{0:T(1024)S(1)}, f32[768]{0:T(1024)}, u32[]{:S(2)}) copy-start(f32[768]{0:T(1024)} %copy-done.16) | copy-start | bytes 9220
  597.6 23.0 %copy-start.22 = (f32[256]{0:T(256)S(1)}, f32[256]{0:T(256)}, u32[]{:S(2)}) copy-start(f32[256]{0:T(256)} %copy-done.21) | copy-start | bytes 3076
  622.9 10.9 %all-to-all-start.10 = ((f32[4,1,4608]{2,1,0:T(1,128)}), f32[4,1,4608]{2,1,0:T(1,128)S(1)}, u32[]{:S(2)}, u32[]{:S(2)}) async-start(f32[4,1,4608]{2,1,0:T(1,128)} %broadcast_in_dim.144), calls=%async_computation.13 | async-start | bytes 147456 | tf_op jit(solution)/shard_map/all_to_all | solution.py:60
  630.1 23.1 %copy-start.31 = (f32[8]{0:T(128)S(1)}, f32[8]{0:T(128)}, u32[]{:S(2)}) copy-start(f32[8]{0:T(128)} %get-tuple-element.36) | copy-start | bytes 100
  644.2 8.9 %all-to-all-start.11 = ((f32[4,8,192]{2,1,0:T(8,128)}), f32[4,8,192]{2,1,0:T(8,128)S(1)}, u32[]{:S(2)}, u32[]{:S(2)}) async-start(f32[4,8,192]{2,1,0:T(8,128)} %broadcast_in_dim.145), calls=%async_computation.14 | async-start | bytes 65536 | tf_op jit(solution)/shard_map/all_to_all | solution.py:60
  (15 other events, 50.4 us)
Sparse Core Ops, SparseCore 0:
  9.6 52.8 all-gather.18
  64.1 28.9 all-gather.12
  113.8 36.0 all-gather.20
  168.4 36.2 all-gather.22
  370.0 34.6 reduce-scatter.5
  410.8 32.5 reduce-scatter.3
  445.3 26.2 all-gather.16
  474.0 23.9 all-gather.14
  546.1 32.7 reduce-scatter.7

commit v2 on v1

--- a/solution.py
+++ b/solution.py
@@ -34,6 +34,10 @@
         0.7978845608028654 * (1.0 + 3.0 * 0.044715 * square)
     )
     return values * half, slope
+
+
+def tie(*values):
+    return lax.optimization_barrier(values)
 
 
 def silu_back(cond, grad_out):
@@ -187,22 +191,89 @@
     )(lengths, projected, grad_attended, projected, logs)
 
 
+def block_of(rows):
+    return 256 if rows % 256 == 0 else rows
+
+
+def dispatch_kernel(target_ref, table_ref, out_ref):
+    block = out_ref.shape[0]
+    slots = pl.program_id(0) * block + lax.broadcasted_iota(
+        jnp.int32, (block, table_ref.shape[0]), 0
+    )
+    hot = slots == target_ref[0:1, :]
+    for j in range(1, target_ref.shape[0]):
+        hot = hot | (slots == target_ref[j : j + 1, :])
+    out_ref[...] = dot(jnp.where(hot, 1.0, 0.0).astype(BF16), table_ref[...]).astype(BF16)
+
+
+def dispatch(target_rows, table, slot_rows):
+    rows, width = table.shape
+    block = block_of(slot_rows)
+    return pl.pallas_call(
+        dispatch_kernel,
+        grid=(slot_rows // block,),
+        in_specs=[
+            pl.BlockSpec(target_rows.shape, lambda i: (0, 0)),
+            pl.BlockSpec((rows, width), lambda i: (0, 0)),
+        ],
+        out_specs=pl.BlockSpec((block, width), lambda i: (i, 0)),
+        out_shape=jax.ShapeDtypeStruct((slot_rows, width), BF16),
+        name="dispatch",
+    )(target_rows, table)
+
+
+def combine_kernel(target_ref, rows_ref, start_ref, out_ref):
+    slots = lax.broadcasted_iota(jnp.int32, (out_ref.shape[0], rows_ref.shape[0]), 1)
+    hot = slots == target_ref[:, 0:1]
+    for j in range(1, target_ref.shape[1]):
+        hot = hot | (slots == target_ref[:, j : j + 1])
+    picked = dot(jnp.where(hot, 1.0, 0.0).astype(BF16), rows_ref[...])
+    out_ref[...] = (picked + start_ref[...]).astype(BF16)
+
+
+def combine(target_pairs, rows, start):
+    patches, width = start.shape
+    block = block_of(patches)
+    return pl.pallas_call(
+        combine_kernel,
+        grid=(patches // block,),
+        in_specs=[
+            pl.BlockSpec((block, target_pairs.shape[1]), lambda i: (i, 0)),
+            pl.BlockSpec(rows.shape, lambda i: (0, 0)),
+            pl.BlockSpec((block, width), lambda i: (i, 0)),
+        ],
+        out_specs=pl.BlockSpec((block, width), lambda i: (i, 0)),
+        out_shape=jax.ShapeDtypeStruct((patches, width), BF16),
+        name="combine",
+    )(target_pairs, rows, start)
+
+
+def out_columns(attended, grad_branch, router_part):
+    columns = jnp.pad(router_part, ((0, -router_part.shape[0] % 128), (0, 0)))
+    return jnp.concatenate([t_dot(attended, grad_branch), columns.T], axis=1)
+
+
 class HeadSplit:
     def __init__(self, tokens, qkv_weight, out_weight, lengths):
         self.hid = lax.axis_size("hid")
         self.items, self.local, self.width = tokens.shape
         self.cols = self.width // self.hid
         self.lengths = lengths
-        own = qkv_weight.shape[0]
-        parts = qkv_weight.reshape(own, 3, self.hid, self.cols).transpose(2, 0, 1, 3)
-        self.qkv = exchange(parts.reshape(self.hid, own, 3 * self.cols), "hid").reshape(
-            self.width, 3 * self.cols
-        )
-        self.out = lax.all_gather(out_weight, "hid", axis=0, tiled=True)
+        dp, rank = lax.axis_size("dp"), lax.axis_index("dp")
+        chunk = qkv_weight.shape[0] // dp
+        rows = lax.dynamic_slice_in_dim(qkv_weight, rank * chunk, chunk, 0)
+        parts = rows.reshape(chunk, 3, self.hid, self.cols).transpose(2, 0, 1, 3)
+        parts = exchange(parts.reshape(self.hid, chunk, 3 * self.cols), "hid")
+        self.qkv = self.in_order(lax.all_gather(parts, "dp"))
+        rows = lax.dynamic_slice_in_dim(out_weight, rank * chunk, chunk, 0)
+        self.out = self.in_order(copies(copies(rows, "hid"), "dp"))
         tokens_all = lax.all_gather(tokens[None], "hid", axis=0, tiled=True)
         self.tokens_all = tokens_all.transpose(1, 0, 2, 3).reshape(
             self.items, self.hid * self.local, self.width
         )
+
+    def in_order(self, parts):
+        return parts.transpose(1, 0, 2, 3).reshape(self.width, parts.shape[-1])
 
     def to_heads(self, rows):
         parts = rows.reshape(self.items, self.local, self.hid, self.cols).transpose(2, 0, 1, 3)
@@ -229,19 +300,21 @@
         self.attended = self.to_rows(attended)
         return dot(self.attended, self.out)
 
-    def backward(self, grad_branch):
-        out_grad = t_dot(self.attended, grad_branch)
+    def backward(self, grad_branch, router_part):
         grad_attended = dot_t(grad_branch, self.out).astype(BF16)
         grad_heads = self.to_heads(grad_attended.reshape(self.items, self.local, self.width))
+        branch_late, grad_heads = tie(grad_branch, grad_heads)
+        out_parts = spread_rows(out_columns(self.attended, branch_late, router_part))
         grad_projected = attend_back(self.projected, grad_heads, self.logs, self.lengths)
+        grad_projected, out_parts = tie(grad_projected, out_parts)
         rows = grad_projected.reshape(-1, 3 * self.cols)
         grad_part = dot_t(rows, self.qkv).astype(BF16)
         grad_part = grad_part.reshape(self.items, self.hid, self.local, self.width)
         grad_in = lax.psum_scatter(
             grad_part.transpose(1, 0, 2, 3), "hid", scatter_dimension=0, tiled=True
         )[0].astype(F32)
-        qkv_grad = t_dot(self.hidden, rows)
-        return grad_in, qkv_grad, out_grad
+        qkv_parts = spread_rows(t_dot(self.hidden, rows))
+        return grad_in, qkv_parts, out_parts
 
     def join_qkv(self, parts):
         chunk = parts.shape[1]
@@ -256,7 +329,7 @@
     def __init__(self, tokens, qkv_weight, out_weight, lengths):
         self.hid = lax.axis_size("hid")
         self.items, self.local, self.width = tokens.shape
-        self.tokens = tokens
+        self.tokens_all = tokens
         self.lengths = lengths
         self.qkv = lax.all_gather(qkv_weight, "hid", axis=0, tiled=True)
         self.out = lax.all_gather(out_weight, "hid", axis=0, tiled=True)
@@ -271,7 +344,7 @@
 
     def forward(self, shift_in, scale_in):
         items, local, width = self.items, self.local, self.width
-        normed, _ = layer_norm(self.tokens.astype(F32))
+        normed, _ = layer_norm(self.tokens_all.astype(F32))
         hidden = (normed * (1.0 + scale_in) + shift_in).astype(BF16)
         self.hidden = hidden.reshape(-1, width)
         projected = dot(self.hidden, self.qkv).astype(BF16).reshape(items, local, 3 * width)
@@ -289,9 +362,9 @@
         self.attended = attended.astype(BF16).reshape(-1, width)
         return dot(self.attended, self.out)
 
-    def backward(self, grad_branch):
+    def backward(self, grad_branch, router_part):
         items, local, width = self.items, self.local, self.width
-        out_grad = t_dot(self.attended, grad_branch)
+        out_parts = spread_rows(out_columns(self.attended, grad_branch, router_part))
         grad_attended = dot_t(grad_branch, self.out).astype(BF16)
         grad_attended = grad_attended.reshape(items, local, HEADS, HDIM)
         soft = jnp.exp(self.scores() - self.log_total)
@@ -318,7 +391,7 @@
             [grad_queries.reshape(items, local, width).astype(BF16), own], axis=-1
         ).reshape(-1, 3 * width)
         grad_in = dot_t(rows, self.qkv).reshape(items, local, width)
-        return grad_in, t_dot(self.hidden, rows), out_grad
+        return grad_in, spread_rows(t_dot(self.hidden, rows)), out_parts
 
     def join_qkv(self, parts):
         return jnp.sum(parts.astype(F32), axis=0).astype(BF16)
@@ -328,15 +401,25 @@
     hid, dp = lax.axis_size("hid"), lax.axis_size("dp")
     rows, cols = grad.shape
     parts = grad.astype(BF16).reshape(hid, dp, rows // (hid * dp), cols).transpose(1, 0, 2, 3)
-    summed = jnp.sum(exchange(parts, "dp").astype(F32), axis=0).astype(BF16)
-    return exchange(summed, "hid")
-
-
-def dp_sum(grad):
+    return jnp.sum(exchange(parts, "dp").astype(F32), axis=0).astype(BF16)
+
+
+def dp_parts(grad):
     dp = lax.axis_size("dp")
     rows, cols = grad.shape
-    parts = exchange(grad.astype(BF16).reshape(dp, rows // dp, cols), "dp")
-    return jnp.sum(parts.astype(F32), axis=0).astype(BF16)
+    return grad.astype(BF16).reshape(dp, rows // dp, cols)
+
+
+def dp_sum(parts):
+    return jnp.sum(exchange(parts, "dp").astype(F32), axis=0).astype(BF16)
+
+
+def dp_sums(parts):
+    if len({each.shape[2] for each in parts}) > 1:
+        return [dp_sum(each) for each in parts]
+    summed = dp_sum(jnp.concatenate(parts, axis=1))
+    sizes = [each.shape[1] for each in parts]
+    return [summed[sum(sizes[:n]) : sum(sizes[: n + 1])] for n in range(len(sizes))]
 
 
 def dp_join(rows):
@@ -376,7 +459,8 @@
 
     split = HeadSplit if HEADS % hid_count == 0 else PatchSplit
     attention = split(tokens, qkv_weight, out_weight, item_lengths)
-    cot_all = lax.all_gather(cotangent[None], "hid", axis=0, tiled=True)
+    cot_late, attention.tokens_all = tie(cotangent, attention.tokens_all)
+    cot_all = lax.all_gather(cot_late[None], "hid", axis=0, tiled=True)
 
     def owned_rows(table, index):
         rows = table.shape[0]
@@ -421,24 +505,22 @@
     )
     slot_of = jnp.sum(jnp.cumsum(expert_hot, axis=0) * expert_hot, axis=1) - 1
     target = pair_routes * capacity + slot_of
-    pair_count = group_rows * top_count
-    pair_of = (
-        jnp.full((slot_rows,), pair_count, jnp.int32)
-        .at[target]
-        .set(jnp.arange(pair_count, dtype=jnp.int32), unique_indices=True, mode="promise_in_bounds")
-    )
-    token_of = pair_of // top_count
-    swapped = jnp.concatenate([group_routes[:, ::-1].reshape(-1), jnp.zeros((1,), jnp.int32)])
-    other_out = swapped.at[pair_of].get(mode="promise_in_bounds").reshape(dp_count, 1, capacity)
-    other = exchange(other_out, "dp").reshape(slot_rows, 1)
     target_pairs = target.reshape(group_rows, top_count)
+    target_rows = target_pairs.T
+    swapped = group_routes[:, ::-1].reshape(-1)
+    slots = jnp.arange(slot_rows, dtype=jnp.int32)
+    other_out = jnp.sum(jnp.where(target[:, None] == slots[None, :], swapped[:, None], 0), axis=0)
+    other = exchange(other_out.reshape(dp_count, 1, capacity), "dp").reshape(slot_rows, 1)
+
+    marks = jnp.stack([time_steps, class_labels], axis=1).astype(F32)
+    notes = lax.all_gather(jnp.concatenate([cond, marks], axis=1), "dp", axis=0, tiled=True)
+    attention.tokens_all, notes, other = tie(attention.tokens_all, notes, other)
 
     grad_rows = (gate_mid[None] * cot_all.astype(F32)).astype(BF16).reshape(group_rows, width)
-    grads_pad = jnp.concatenate([grad_rows, jnp.zeros((8, width), BF16)], axis=0)
-    send_grads = grads_pad.at[token_of].get(mode="promise_in_bounds")
-    expert_grads = exchange(send_grads.reshape(dp_count, capacity, width), "dp").reshape(
-        slot_rows, width
-    )
+    send_grads = dispatch(target_rows, grad_rows, slot_rows)
+
+    def to_slots(rows):
+        return exchange(rows.reshape(dp_count, capacity, width), "dp").reshape(slot_rows, width)
 
     tokens_f = tokens.astype(F32)
     normed_in, inverse_in = layer_norm(tokens_f)
@@ -446,19 +528,25 @@
     residual = tokens_f + gate_in * branch
     normed_mid, inverse_mid = layer_norm(residual)
     hidden_mid = (normed_mid * (1.0 + scale_mid) + shift_mid).astype(BF16)
+    hidden_mid, send_grads = tie(hidden_mid, send_grads)
+    expert_grads = to_slots(send_grads)
     mid_rows = lax.all_gather(hidden_mid[None], "hid", axis=0, tiled=True).reshape(
         group_rows, width
     )
-    send_rows = mid_rows.at[jnp.minimum(token_of, group_rows - 1)].get(mode="promise_in_bounds")
-    expert_rows = exchange(send_rows.reshape(dp_count, capacity, width), "dp").reshape(
-        slot_rows, width
-    )
+    send_rows, expert_grads = tie(dispatch(target_rows, mid_rows, slot_rows), expert_grads)
+    expert_rows = to_slots(send_rows)
 
     shared_gelu, shared_slope = gelu_pair(dot(mid_rows, shared_up))
     shared_act = shared_gelu.astype(BF16)
     grad_shared_pre = (dot_t(grad_rows, shared_down) * shared_slope).astype(BF16)
     grad_mid_part = dot_t(grad_shared_pre, shared_up)
     shared_out = dot(shared_act, shared_down)
+    down_parts = dp_parts(t_dot(shared_act, grad_rows))
+    up_parts = dp_parts(t_dot(mid_rows, grad_shared_pre))
+    expert_rows, down_parts, up_parts, grad_mid_part, shared_out = tie(
+        expert_rows, down_parts, up_parts, grad_mid_part, shared_out
+    )
+    shared_down_rows, shared_up_rows = dp_sums([down_parts, up_parts])
 
     up, down = expert_up[0], expert_down[0]
     logits = dot_t(expert_rows, router_rows)
@@ -479,32 +567,29 @@
     slot_grads = (
         dot_t(grad_expert_pre, up) + dot(logits_high, router_rows) + dot(logits_low, router_rows)
     ).astype(BF16)
-    back_rows = exchange(slot_grads.reshape(dp_count, capacity, width), "dp").reshape(
-        slot_rows, width
-    )
+    slot_grads, shared_down_rows, shared_up_rows = tie(
+        slot_grads, shared_down_rows, shared_up_rows
+    )
+    back_rows = to_slots(slot_grads)
     expert_act = (gate * expert_gelu).astype(BF16)
     expert_out = dot(expert_act, down).astype(BF16)
-    returned = exchange(expert_out.reshape(dp_count, capacity, width), "dp").reshape(
-        slot_rows, width
-    )
-    router_part = t_dot(logits_high, expert_rows) + t_dot(logits_low, expert_rows)
     expert_down_grad = t_dot(expert_act, expert_grads)[None]
     expert_up_grad = t_dot(expert_rows, grad_expert_pre)[None]
-    shared_down_rows = dp_sum(t_dot(shared_act, grad_rows))
-    shared_up_rows = dp_sum(t_dot(mid_rows, grad_shared_pre))
-
-    def combine(rows, start):
-        total = start
-        for j in range(top_count):
-            total = total + rows.at[target_pairs[:, j]].get(mode="promise_in_bounds").astype(F32)
+    router_part = t_dot(logits_high, expert_rows) + t_dot(logits_low, expert_rows)
+    back_rows, expert_out, expert_down_grad, expert_up_grad, router_part = tie(
+        back_rows, expert_out, expert_down_grad, expert_up_grad, router_part
+    )
+    returned = to_slots(expert_out)
+
+    def own_patches(rows):
         return lax.psum_scatter(
-            total.astype(BF16).reshape(hid_count, item_count, local_len, width),
+            rows.reshape(hid_count, item_count, local_len, width),
             "hid",
             scatter_dimension=0,
             tiled=True,
         )[0].astype(F32)
 
-    grad_mid = combine(back_rows, grad_mid_part)
+    grad_mid = own_patches(combine(target_pairs, back_rows, grad_mid_part))
     grad_out = cotangent.astype(F32)
     grad_scale_mid = jnp.sum(grad_mid * normed_mid, axis=1)
     grad_shift_mid = jnp.sum(grad_mid, axis=1)
@@ -512,11 +597,12 @@
     grad_gate_in = jnp.sum(grad_residual * branch, axis=1)
     grad_branch = (gate_in * grad_residual).astype(BF16).reshape(row_count, width)
 
-    moe = combine(returned, shared_out)
+    returned, _ = tie(returned, grad_branch)
+    moe = own_patches(combine(target_pairs, returned, shared_out))
     output = (residual + gate_mid * moe).astype(BF16)
     grad_gate_mid = jnp.sum(grad_out * moe, axis=1)
 
-    grad_in, qkv_grad, out_grad = attention.backward(grad_branch)
+    grad_in, qkv_parts, out_parts = attention.backward(grad_branch, router_part)
     grad_scale_in = jnp.sum(grad_in * normed_in, axis=1)
     grad_shift_in = jnp.sum(grad_in, axis=1)
     tokens_grad = grad_residual + norm_back(grad_in * (1.0 + scale_in), normed_in, inverse_in)
@@ -526,8 +612,6 @@
         axis=1,
     ).reshape(item_count, 6 * width)
     shifts_all = lax.all_gather(small_sum(grad_shifts, "hid"), "dp", axis=0, tiled=True)
-    marks = jnp.stack([time_steps, class_labels], axis=1).astype(F32)
-    notes = lax.all_gather(jnp.concatenate([cond, marks], axis=1), "dp", axis=0, tiled=True)
     cond_own = lax.dynamic_slice_in_dim(notes[:, :width], hid_rank * own_width, own_width, 1)
     scaled_all = jax.nn.silu(cond_own).astype(BF16).astype(F32)
     modulation_grad = exact_dot(scaled_all.T, shifts_all)
@@ -542,20 +626,21 @@
     time_grad = table_grad(time_table, notes[:, width])
     class_grad = table_grad(class_table, notes[:, width + 1])
 
-    router_sum = small_sum(small_sum(router_part, "hid"), "dp")
-    router_grad = lax.dynamic_slice_in_dim(router_sum, hid_rank * own_width, own_width, 1).T
-
-    out_rows = jnp.sum(spread_rows(out_grad).astype(F32), axis=0).astype(BF16)
-    qkv_rows = attention.join_qkv(spread_rows(qkv_grad))
+    blocks = exchange(jnp.concatenate([qkv_parts, out_parts], axis=2), "hid")
+    qkv_cols = qkv_parts.shape[2]
+    out_rows = jnp.sum(blocks[:, :, qkv_cols:].astype(F32), axis=0).astype(BF16)
+    qkv_rows = attention.join_qkv(blocks[:, :, :qkv_cols])
+    joined = dp_join(jnp.concatenate([qkv_rows, out_rows], axis=1))
+    qkv_size = 3 * width
     return (
         output,
         tokens_grad,
         time_grad,
         class_grad,
         modulation_grad,
-        dp_join(qkv_rows),
-        dp_join(out_rows),
-        router_grad,
+        joined[:, :qkv_size],
+        joined[:, qkv_size : qkv_size + width],
+        joined[:, qkv_size + width : qkv_size + width + dp_count],
         dp_join(shared_up_rows),
         dp_join(shared_down_rows),
         expert_up_grad,

time: 672 us -> 595 us (0.89)
  local copies, waits for them, and re-layouts: 103 us -> 39.1 us
  blocking collectives: 67.7 us -> 28.6 us
  Pallas kernels: 27.8 us -> 63.8 us
  matrix products: 117 us -> 103 us
    gather x7 -> x0, local copies, waits for them, and re-layouts: 66.8 us -> none  [the longest x4 32.8 us: combine(): rows.at[target_pairs[:, j]].get(mode='promise_in_bounds').astype(F32)]
    all_gather x2 -> x1, waiting for transfers between devices: 37.9 us -> 0.01 us  [shards(): cot_all = lax.all_gather(cot_late[None], 'hid', axis=0, tiled=True)]
    pallas_call x0 -> x4, Pallas kernels: none -> 35.6 us  [the longest x2 18 us: dispatch(): pl.pallas_call(dispatch_kernel, grid=(slot_rows // block,), in_specs=[pl....]
    all_gather x1, waiting for transfers between devices: 4.85 us -> 38.4 us  [shards(): lax.all_gather(hidden_mid[None], 'hid', axis=0, tiled=True)]
    reduce_scatter x2, waiting for transfers between devices: 0.02 us -> 26.7 us  [own_patches(): lax.psum_scatter(rows.reshape(hid_count, item_count, local_len, width), '...]
    all_to_all x1 -> x0, blocking collectives: 20.3 us -> none  [exchange(): return lax.all_to_all(values, axis, split_axis=0, concat_axis=0, tiled=True)]
    all_gather x1, waiting for transfers between devices: 18.7 us -> 0.01 us  [__init__(): tokens_all = lax.all_gather(tokens[None], 'hid', axis=0, tiled=True)]
    all_gather x1, blocking collectives: 19.9 us -> 8.75 us  [shards(): lax.all_gather(jnp.concatenate([cond, marks], axis=1), 'dp', axis=0, tile...]
  transfers between devices with their start and end apart: 28 -> 27, of which waited for: 16 -> 16; matrix products, arithmetic and copies ran while one was open for 35% -> 29% of each run, Pallas kernels for 4% -> 8%
where the time goes in v2:
time: 595 us; the launch traced here: 584 us
  waiting for transfers between devices  209 us (35%)
  matrix products  103 us (17%)
  starting transfers between devices  77.5 us (13%)
  Pallas kernels  63.8 us (11%)
  other arithmetic  46.1 us (8%)
  local copies, waits for them, and re-layouts  39.1 us (7%)
  blocking collectives  28.6 us (5%)
  between operations  17.3 us (3%)
    all_to_all x18, waiting for transfers between devices, exchange(): return lax.all_to_all(values, axis, split_axis=0, concat_axis=0, tiled=True)  141 us
    all_to_all x18, starting transfers between devices, exchange(): return lax.all_to_all(values, axis, split_axis=0, concat_axis=0, tiled=True)  77.1 us
    all_gather x1, waiting for transfers between devices, shards(): lax.all_gather(hidden_mid[None], 'hid', axis=0, tiled=True)  38.4 us
    dot_general x8, matrix products, t_dot(): lax.dot_general(left, right, (((0,), (0,)), ((), ())), preferred_element_...  34.4 us
    dot_general x7, matrix products, dot_t(): lax.dot_general(left, right, (((1,), (1,)), ((), ())), preferred_element_...  30.4 us
    dot_general x9, matrix products, dot(): return jnp.dot(left, right, preferred_element_type=F32)  30.2 us
    reduce_scatter x2, waiting for transfers between devices, own_patches(): lax.psum_scatter(rows.reshape(hid_count, item_count, local_len, width), '...  26.7 us
    pallas_call x2, Pallas kernels, dispatch(): pl.pallas_call(dispatch_kernel, grid=(slot_rows // block,), in_specs=[pl....  18 us
  transfers between devices with their start and end apart: 27, of which 16 were waited for; matrix products, arithmetic and copies ran while one was open for 29% of the time, Pallas kernels for 8%

profile of v2, /device:TPU:0, one launch (start us, length us, event | category | flops | bytes accessed | tf_op | source)
XLA Modules:
  0.0 584.0 jit_solution(10232802017472050931)
XLA Ops:
  13.3 3.7 select_reduce_fusion
  17.7 5.2 all-to-all-start.2
  28.2 4.9 all-to-all-start
  34.1 5.1 all-to-all-done
  45.8 6.3 %all-to-all-done.3 = bf16[4,24,576]{2,1,0:T(8,128)(2,1)S(1)} async-done(((bf16[4,24,576]{2,1,0:T(8,128)(2,1)}), bf16[4,24,576]{2,1,0:T(8,128)(2,1)S(1)}, u32[]{:S(2)}, u32[]{:S(2)}) %all-to-all-start.3) | async-done | bytes 110624 | tf_op jit(solution)/shard_map/all_to_all | solution.py:64
  56.7 5.4 all-to-all-done.5
  66.2 8.8 %all-gather.5 = f32[8,1,770]{2,1,0:T(1,128)S(1)} all-gather(f32[1,1,770]{2,1,0:T(1,128)S(1)} %maximum_bitcast_fusion.1), channel_id=1, replica_groups=mesh['dp'=8,'hid'=4] {'dp'}, dimensions={0}, use_global_device_ids=true | all-gather | bytes 27720 | tf_op jit(solution)/shard_map/all_gather | solution.py:516
  75.5 10.3 %all-gather.1 = bf16[32,24,576]{2,1,0:T(8,128)(2,1)S(1)} all-gather(bf16[4,24,576]{2,1,0:T(8,128)(2,1)S(1)} %all-to-all-done.3), channel_id=3, replica_groups=mesh['dp'=8,'hid'=4] {'dp'}, dimensions={0}, use_global_device_ids=true | all-gather | bytes 995328 | tf_op jit(solution)/shard_map/all_gather | solution.py:267
  88.2 4.2 all-to-all-start.6
  100.0 13.1 %attend.1 = (bf16[1,1024,192]{2,1,0:T(8,128)(2,1)}, f32[1,8,1024]{2,1,0:T(8,128)}) custom-call(s32[1]{0:T(128)S(6)} %copy.166.length_ref, bf16[1,1024,576]{2,1,0:T(8,128)(2,1)} %fusion.9.query_ref.all_ref, bf16[1,1024,576]{2,1,0:T(8,128)(2,1)} %fusion.9.query_ref.all_ref), custom_call_target="tpu_custom_call" | custom-call | tf_op jit(solution)/shard_map/attend/pallas_call | solution.py:145
  115.1 5.3 all-to-all-start.4
  124.8 16.9 %all-to-all-done.4 = bf16[4,1,256,192]{2,3,1,0:T(8,128)(2,1)} async-done(((bf16[4,1,256,192]{2,3,1,0:T(8,128)(2,1)}), bf16[4,1,256,192]{2,3,1,0:T(8,128)(2,1)}, u32[]{:S(2)}, u32[]{:S(2)}) %all-to-all-start.4) | async-done | bytes 393248 | tf_op jit(solution)/shard_map/all_to_all | solution.py:64
  141.7 3.4 fusion.108
  149.1 9.0 %dispatch.2 = bf16[2560,768]{1,0:T(8,128)(2,1)} custom-call(s32[2,1024]{1,0:T(2,128)} %copy.129.target_ref, bf16[1024,768]{1,0:T(8,128)(2,1)} %bitcast.238), custom_call_target="tpu_custom_call" | custom-call | tf_op jit(solution)/shard_map/dispatch/pallas_call | solution.py:212
  158.1 4.5 all-to-all-start.7
  163.3 38.4 %all-gather.24.cloned.1.call-done = bf16[4,256,768]{2,1,0:T(8,128)(2,1)} async-done(((bf16[1,256,768]{2,1,0:T(8,128)(2,1)}), bf16[4,256,768]{2,1,0:T(8,128)(2,1)}) %all-gather.24.cloned.1.call-update) | async-done | bytes 1572880 | tf_op jit(solution)/shard_map/all_gather | solution.py:533
  201.8 9.0 %dispatch.3 = bf16[2560,768]{1,0:T(8,128)(2,1)} custom-call(s32[2,1024]{1,0:T(2,128)} %copy.129.target_ref, bf16[1024,768]{1,0:T(8,128)(2,1)} %bitcast.247), custom_call_target="tpu_custom_call" | custom-call | tf_op jit(solution)/shard_map/dispatch/pallas_call | solution.py:212
  210.8 4.5 all-to-all-start.8
  227.7 3.6 fusion.107.start_ref
  234.3 27.3 %all-to-all-done.8 = bf16[8,320,768]{2,1,0:T(8,128)(2,1)} async-done(((bf16[8,320,768]{2,1,0:T(8,128)(2,1)}), bf16[8,320,768]{2,1,0:T(8,128)(2,1)}, u32[]{:S(2)}, u32[]{:S(2)}) %all-to-all-start.8) | async-done | bytes 3932192 | tf_op jit(solution)/shard_map/all_to_all | solution.py:64
  264.8 4.8 all-to-all-start.9
  273.0 5.6 fusion.14
  278.7 10.7 %multiply_reduce_fusion = (f32[2560]{0:T(1024)S(1)}, bf16[2560,768]{0,1:T(8,128)(2,1)S(1)}) fusion(f32[2560,768]{0,1:T(8,128)S(1)} %fusion.14, f32[2560]{0:T(1024)S(1)} %fusion.88, bf16[2560,768]{1,0:T(8,128)(2,1)} %bitcast.32, bf16[1,768,768]{2,1,0:T(8,128)(2,1)S(1)} %copy-done.30), kind=kOutput, calls=%fused_computation.4 | convolution fusion | flops 3063150080 | bytes 16928768 | tf_op jit(solution)/shard_map/dot_general | solution.py:56
  289.4 4.2 fusion.70
  304.2 4.5 all-to-all-start.10
  311.8 8.1 %convolution_bitcast_fusion = f32[1,768,768]{2,1,0:T(8,128)} fusion(bf16[2560,768]{1,0:T(8,128)(2,1)} %bitcast.35, bf16[2560,768]{0,1:T(8,128)(2,1)} %copy-done.33), kind=kOutput, calls=%fused_computation.29 | convolution fusion | flops 3019898880 | bytes 10223616 | tf_op jit(solution)/shard_map/dot_general | solution.py:60
  319.9 6.6 %convolution_convert_fusion = bf16[2560,768]{1,0:T(8,128)(2,1)} fusion(bf16[1,768,768]{2,1,0:T(8,128)(2,1)S(1)} %copy-done.31, f32[2560]{0:T(1024)S(1)} %fusion.88, f32[2560,768]{0,1:T(8,128)S(1)} %bitcast.265), kind=kOutput, calls=%fused_computation.10 | convolution fusion | flops 3041525760 | bytes 12986368 | tf_op jit(solution)/shard_map/dot_general | solution.py:52
  326.5 8.2 %convolution_bitcast_fusion.1 = f32[1,768,768]{2,1,0:T(8,128)} fusion(bf16[2560,768]{1,0:T(8,128)(2,1)} %bitcast.32, f32[2560]{0:T(1024)S(1)} %fusion.88, f32[2560,768]{0,1:T(8,128)S(1)} %bitcast.265), kind=kOutput, calls=%fused_computation.30 | convolution fusion | flops 3039559680 | bytes 14166016 | tf_op jit(solution)/shard_map/dot_general | solution.py:60
  334.7 20.4 %all-to-all-done.10 = bf16[8,320,768]{2,1,0:T(8,128)(2,1)} async-done(((bf16[8,320,768]{2,1,0:T(8,128)(2,1)}), bf16[8,320,768]{2,1,0:T(8,128)(2,1)}, u32[]{:S(2)}, u32[]{:S(2)}) %all-to-all-start.10) | async-done | bytes 3932192 | tf_op jit(solution)/shard_map/all_to_all | solution.py:64
  355.1 8.8 %combine.2 = bf16[1024,768]{1,0:T(8,128)(2,1)} custom-call(s32[1024,2]{1,0:T(8,128)} %copy-done.2, bf16[2560,768]{1,0:T(8,128)(2,1)} %bitcast.40.rows_ref, f32[1024,768]{1,0:T(8,128)} %fusion.111.start_ref), custom_call_target="tpu_custom_call" | custom-call | tf_op jit(solution)/shard_map/combine/pallas_call | solution.py:237
  364.5 4.7 all-to-all-start.11
  369.9 26.7 %reduce-scatter.4.cloned.1.call-done = bf16[1,1,256,768]{3,2,1,0:T(8,128)(2,1)} async-done(((bf16[4,1,256,768]{3,2,1,0:T(8,128)(2,1)}), bf16[1,1,256,768]{3,2,1,0:T(8,128)(2,1)}) %reduce-scatter.4.cloned.1.call-update) | async-done | bytes 393232 | tf_op jit(solution)/shard_map/reduce_scatter | solution.py:585
  401.7 15.4 %all-to-all-done.11 = bf16[8,320,768]{2,1,0:T(8,128)(2,1)} async-done(((bf16[8,320,768]{2,1,0:T(8,128)(2,1)}), bf16[8,320,768]{2,1,0:T(8,128)(2,1)}, u32[]{:S(2)}, u32[]{:S(2)}) %all-to-all-start.11) | async-done | bytes 3932192 | tf_op jit(solution)/shard_map/all_to_all | solution.py:64
  417.1 8.8 %combine.3 = bf16[1024,768]{1,0:T(8,128)(2,1)} custom-call(s32[1024,2]{1,0:T(8,128)} %copy-done.2, bf16[2560,768]{1,0:T(8,128)(2,1)} %bitcast.44.rows_ref, f32[1024,768]{1,0:T(8,128)} %fusion.107.start_ref), custom_call_target="tpu_custom_call" | custom-call | tf_op jit(solution)/shard_map/combine/pallas_call | solution.py:237
  430.4 4.1 all-to-all-start.12
  435.4 8.2 %all-to-all-done.12 = bf16[4,1,256,192]{2,3,1,0:T(8,128)(2,1)} async-done(((bf16[4,1,256,192]{2,3,1,0:T(8,128)(2,1)}), bf16[4,1,256,192]{2,3,1,0:T(8,128)(2,1)}, u32[]{:S(2)}, u32[]{:S(2)}) %all-to-all-start.12) | async-done | bytes 393248 | tf_op jit(solution)/shard_map/all_to_all | solution.py:64
  449.3 5.2 all-to-all-start.13
  454.5 15.1 %attend_back.1 = bf16[1,1024,576]{2,1,0:T(8,128)(2,1)} custom-call(s32[1]{0:T(128)S(6)} %copy.166.length_ref, bf16[1,1024,576]{2,1,0:T(8,128)(2,1)} %fusion.9.query_ref.all_ref, bf16[1,1024,192]{2,1,0:T(8,128)(2,1)} %bitcast.244, bf16[1,1024,576]{2,1,0:T(8,128)(2,1)} %fusion.9.query_ref.all_ref, f32[1,8,1024]{2,1,0:T(8,128)} %get-tuple-element.61.log_ref), custom_call_target="tpu_custom_call" | custom-call | tf_op jit(solution)/shard_map/attend_back/pallas_call | solution.py:172
  469.6 3.9 all-to-all-done.13
  475.0 4.2 convolution_convert_fusion.1
  479.3 4.2 convolution_convert_fusion.6
  487.9 4.2 all-to-all-start.16
  492.2 14.7 %all-to-all-done.16 = bf16[8,4,24,576]{3,2,1,0:T(8,128)(2,1)} async-done(((bf16[8,4,24,576]{3,2,1,0:T(8,128)(2,1)}), bf16[8,4,24,576]{3,2,1,0:T(8,128)(2,1)}, u32[]{:S(2)}, u32[]{:S(2)}) %all-to-all-start.16) | async-done | bytes 884768 | tf_op jit(solution)/shard_map/all_to_all | solution.py:64
  509.0 4.1 all-to-all-start.17
  519.3 10.5 %all-to-all-done.17 = bf16[4,24,1472]{2,1,0:T(8,128)(2,1)} async-done(((bf16[4,24,1472]{2,1,0:T(8,128)(2,1)}), bf16[4,24,1472]{2,1,0:T(8,128)(2,1)}, u32[]{:S(2)}, u32[]{:S(2)}) %all-to-all-start.17) | async-done | bytes 282656 | tf_op jit(solution)/shard_map/all_to_all | solution.py:64
  547.4 9.6 %all-gather.6 = f32[8,1,4608]{2,1,0:T(1,128)S(1)} all-gather(f32[1,1,4608]{2,1,0:T(1,128)S(1)} %reshape.761), channel_id=6, replica_groups=mesh['dp'=8,'hid'=4] {'dp'}, dimensions={0}, use_global_device_ids=true | all-gather | bytes 165888 | tf_op jit(solution)/shard_map/all_gather | solution.py:614
  559.1 3.6 all-to-all-start.15
  562.7 3.5 fusion.49
  (244 shorter events, 145.4 us)
Async XLA Ops:
  7.2 48.9 %copy-start = (bf16[192,4608]{1,0:T(8,128)(2,1)S(1)}, bf16[192,4608]{1,0:T(8,128)(2,1)}, u32[]{:S(2)}) copy-start(bf16[192,4608]{1,0:T(8,128)(2,1)} %param.26) | copy-start | bytes 5308420
  7.2 25.9 %copy-start.22 = (bf16[192,8]{0,1:T(8,128)(2,1)S(1)}, bf16[192,8]{0,1:T(8,128)(2,1)}, u32[]{:S(2)}) copy-start(bf16[192,8]{0,1:T(8,128)(2,1)} %param.29) | copy-start | bytes 9220
  7.2 86.2 %all-gather.20.cloned.1.call-start = ((), (), s32[]{:S(2)}) async-start(), calls=%async_computation.27 | async-start | bytes 1966080 | tf_op jit(solution)/shard_map/all_gather | solution.py:270
  17.7 9.9 %all-to-all-start.2 = ((s32[8,1,320]{2,1,0:T(1,128)}), s32[8,1,320]{2,1,0:T(1,128)S(1)}, u32[]{:S(2)}, u32[]{:S(2)}) async-start(s32[8,1,320]{2,1,0:T(1,128)} %reshape.685), calls=%async_computation.2 | async-start | bytes 24576 | tf_op jit(solution)/shard_map/all_to_all | solution.py:64
  28.2 11.0 %all-to-all-start = ((f32[4,1,768]{2,1,0:T(1,128)}), f32[4,1,768]{2,1,0:T(1,128)S(1)}, u32[]{:S(2)}, u32[]{:S(2)}) async-start(f32[4,1,768]{2,1,0:T(1,128)} %broadcast_in_dim.130), calls=%async_computation | async-start | bytes 24576 | tf_op jit(solution)/shard_map/all_to_all | solution.py:64
  39.2 12.9 %all-to-all-start.3 = ((bf16[4,24,576]{2,1,0:T(8,128)(2,1)}), bf16[4,24,576]{2,1,0:T(8,128)(2,1)S(1)}, u32[]{:S(2)}, u32[]{:S(2)}) async-start(bf16[4,24,576]{2,1,0:T(8,128)(2,1)} %reshape.689), calls=%async_computation.3 | async-start | bytes 245760 | tf_op jit(solution)/shard_map/all_to_all | solution.py:64
  52.8 9.3 %all-to-all-start.5 = ((bf16[4,24,768]{2,1,0:T(8,128)(2,1)}), bf16[4,24,768]{2,1,0:T(8,128)(2,1)S(1)}, u32[]{:S(2)}, u32[]{:S(2)}) async-start(bf16[4,24,768]{2,1,0:T(8,128)(2,1)} %broadcast_in_dim.138), calls=%async_computation.5 | async-start | bytes 294912 | tf_op jit(solution)/shard_map/all_to_all | solution.py:64
  62.0 23.8 %copy-start.10 = (bf16[4,24,768]{2,1,0:T(8,128)(2,1)}, bf16[4,24,768]{2,1,0:T(8,128)(2,1)S(1)}, u32[]{:S(2)}) copy-start(bf16[4,24,768]{2,1,0:T(8,128)(2,1)S(1)} %all-to-all-done.5) | copy-start | bytes 442372
  62.8 23.1 %all-to-all-start.1 = ((f32[4,1,10752]{2,1,0:T(1,128)}), f32[4,1,10752]{2,1,0:T(1,128)S(1)}, u32[]{:S(2)}, u32[]{:S(2)}) async-start(f32[4,1,10752]{2,1,0:T(1,128)} %broadcast_in_dim.133), calls=%async_computation.1 | async-start | bytes 344064 | tf_op jit(solution)/shard_map/all_to_all | solution.py:64
  85.9 11.3 %copy-start.9 = (bf16[8,4,24,576]{3,2,0,1:T(8,128)(2,1)}, bf16[8,4,24,576]{3,2,0,1:T(8,128)(2,1)S(1)}, u32[]{:S(2)}) copy-start(bf16[8,4,24,576]{3,2,0,1:T(8,128)(2,1)S(1)} %copy.123) | copy-start | bytes 2654212
  88.2 26.9 %all-to-all-start.6 = ((bf16[8,4,24,768]{3,2,1,0:T(8,128)(2,1)}), bf16[8,4,24,768]{3,2,1,0:T(8,128)(2,1)}, u32[]{:S(2)}, u32[]{:S(2)}) async-start(bf16[8,4,24,768]{3,2,1,0:T(8,128)(2,1)} %broadcast_in_dim.139), calls=%async_computation.6 | async-start | bytes 2359296 | tf_op jit(solution)/shard_map/all_to_all | solution.py:64
  92.4 53.8 %all-gather.22.cloned.1.call-start = ((), (), s32[]{:S(2)}) async-start(), calls=%async_computation.28 | async-start | bytes 1966080 | tf_op jit(solution)/shard_map/all_gather | solution.py:463
  93.4 6.6 %copy-start.25 = (f32[768]{0:T(1024)}, f32[768]{0:T(1024)S(1)}, u32[]{:S(2)}) copy-start(f32[768]{0:T(1024)S(1)} %get-tuple-element.165) | copy-start | bytes 9220
  93.4 52.9 %copy-start.12 = (f32[768]{0:T(1024)}, f32[768]{0:T(1024)S(1)}, u32[]{:S(2)}) copy-start(f32[768]{0:T(1024)S(1)} %get-tuple-element.162) | copy-start | bytes 9220
  100.0 22.2 %copy-start.1 = (bf16[1,256,768]{2,1,0:T(8,128)(2,1)S(1)}, bf16[1,256,768]{2,1,0:T(8,128)(2,1)}, u32[]{:S(2)}) copy-start(bf16[1,256,768]{2,1,0:T(8,128)(2,1)} %param.18) | copy-start | bytes 1179652
  115.1 26.6 %all-to-all-start.4 = ((bf16[4,1,256,192]{2,3,1,0:T(8,128)(2,1)}), bf16[4,1,256,192]{2,3,1,0:T(8,128)(2,1)}, u32[]{:S(2)}, u32[]{:S(2)}) async-start(bf16[4,1,256,192]{2,3,1,0:T(8,128)(2,1)} %copy.125), calls=%async_computation.4 | async-start | bytes 786432 | tf_op jit(solution)/shard_map/all_to_all | solution.py:64
  121.5 23.6 %copy-start.2 = (s32[1024,2]{1,0:T(8,128)}, s32[1024,2]{1,0:T(8,128)S(1)}, u32[]{:S(2)}) copy-start(s32[1024,2]{1,0:T(8,128)S(1)} %multiply_add_fusion.target_ref) | copy-start | bytes 24580
  122.4 22.8 %copy-start.14 = (f32[256]{0:T(256)}, f32[256]{0:T(256)S(1)}, u32[]{:S(2)}) copy-start(f32[256]{0:T(256)S(1)} %broadcast_multiply_fusion.3) | copy-start | bytes 3076
  122.4 22.9 %copy-start.20 = (f32[768]{0:T(1024)S(1)}, f32[768]{0:T(1024)}, u32[]{:S(2)}) copy-start(f32[768]{0:T(1024)} %get-tuple-element.163) | copy-start | bytes 9220
  158.1 52.7 %all-to-all-start.7 = ((bf16[8,320,768]{2,1,0:T(8,128)(2,1)}), bf16[8,320,768]{2,1,0:T(8,128)(2,1)}, u32[]{:S(2)}, u32[]{:S(2)}) async-start(bf16[8,320,768]{2,1,0:T(8,128)(2,1)} %bitcast.227), calls=%async_computation.7 | async-start | bytes 7864320 | tf_op jit(solution)/shard_map/all_to_all | solution.py:64
  162.6 39.2 %all-gather.24.cloned.1.call-start = ((), (), s32[]{:S(2)}) async-start(), calls=%async_computation.29 | async-start | bytes 1966080 | tf_op jit(solution)/shard_map/all_gather | solution.py:533
  210.8 50.8 %all-to-all-start.8 = ((bf16[8,320,768]{2,1,0:T(8,128)(2,1)}), bf16[8,320,768]{2,1,0:T(8,128)(2,1)}, u32[]{:S(2)}, u32[]{:S(2)}) async-start(bf16[8,320,768]{2,1,0:T(8,128)(2,1)} %bitcast.226), calls=%async_computation.8 | async-start | bytes 7864320 | tf_op jit(solution)/shard_map/all_to_all | solution.py:64
  264.8 36.6 %all-to-all-start.9 = ((bf16[8,192,768]{2,1,0:T(8,128)(2,1)}), bf16[8,192,768]{2,1,0:T(8,128)(2,1)}, u32[]{:S(2)}, u32[]{:S(2)}) async-start(bf16[8,192,768]{2,1,0:T(8,128)(2,1)} %pad_maximum_fusion), calls=%async_computation.9 | async-start | bytes 4718592 | tf_op jit(solution)/shard_map/all_to_all | solution.py:64
  278.6 10.7 %copy-start.32 = (f32[2560,768]{0,1:T(8,128)}, f32[2560,768]{0,1:T(8,128)S(1)}, u32[]{:S(2)}) copy-start(f32[2560,768]{0,1:T(8,128)S(1)} %fusion.14) | copy-start | bytes 23592964
  304.2 50.8 %all-to-all-start.10 = ((bf16[8,320,768]{2,1,0:T(8,128)(2,1)}), bf16[8,320,768]{2,1,0:T(8,128)(2,1)}, u32[]{:S(2)}, u32[]{:S(2)}) async-start(bf16[8,320,768]{2,1,0:T(8,128)(2,1)} %bitcast.225), calls=%async_computation.10 | async-start | bytes 7864320 | tf_op jit(solution)/shard_map/all_to_all | solution.py:64
  308.8 87.8 %reduce-scatter.4.cloned.1.call-start = ((), (), s32[]{:S(2)}) async-start(), calls=%async_computation.21 | async-start | bytes 1966080 | tf_op jit(solution)/shard_map/reduce_scatter | solution.py:585
  308.8 11.1 %slice-start = ((s8[7864320]{0:T(1024)(128)(4,1)}), s8[4194304]{0:T(1024)(128)(4,1)S(1)}, s32[]{:S(2)}) async-start(s8[7864320]{0:T(1024)(128)(4,1)} %bitcast.264), calls=%async_computation.30 | async-start | bytes 8388608
  311.8 8.1 %copy-start.31 = (bf16[1,768,768]{2,1,0:T(8,128)(2,1)S(1)}, bf16[1,768,768]{2,1,0:T(8,128)(2,1)}, u32[]{:S(2)}) copy-start(bf16[1,768,768]{2,1,0:T(8,128)(2,1)} %param.33) | copy-start | bytes 3538948
  311.8 8.1 %slice-start.1 = ((s8[7864320]{0:T(1024)(128)(4,1)}), s8[3670016]{0:T(1024)(128)(4,1)S(1)}, s32[]{:S(2)}) async-start(s8[7864320]{0:T(1024)(128)(4,1)} %bitcast.264), calls=%async_computation.31 | async-start | bytes 7340032
  363.9 149.5 %all-gather.18.cloned.1.call-start = ((), (), s32[]{:S(2)}) async-start(), calls=%async_computation.26 | async-start | bytes 1327104 | tf_op jit(solution)/shard_map/all_gather | solution.py:426
  364.5 34.1 %copy-start.7 = (bf16[1,256,768]{2,1,0:T(8,128)(2,1)S(1)}, bf16[1,256,768]{2,1,0:T(8,128)(2,1)}, u32[]{:S(2)}) copy-start(bf16[1,256,768]{2,1,0:T(8,128)(2,1)} %param.19) | copy-start | bytes 1179652
  364.5 52.6 %all-to-all-start.11 = ((bf16[8,320,768]{2,1,0:T(8,128)(2,1)}), bf16[8,320,768]{2,1,0:T(8,128)(2,1)}, u32[]{:S(2)}, u32[]{:S(2)}) async-start(bf16[8,320,768]{2,1,0:T(8,128)(2,1)} %bitcast.242), calls=%async_computation.11 | async-start | bytes 7864320 | tf_op jit(solution)/shard_map/all_to_all | solution.py:64
  369.3 147.1 %all-gather.16.cloned.1.call-start = ((), (), s32[]{:S(2)}) async-start(), calls=%async_computation.25 | async-start | bytes 1327104 | tf_op jit(solution)/shard_map/all_gather | solution.py:426
  369.8 163.1 %reduce-scatter.6.cloned.1.call-start = ((), (), s32[]{:S(2)}) async-start(), calls=%async_computation.22 | async-start | bytes 1966080 | tf_op jit(solution)/shard_map/reduce_scatter | solution.py:585
  430.4 13.2 %all-to-all-start.12 = ((bf16[4,1,256,192]{2,3,1,0:T(8,128)(2,1)}), bf16[4,1,256,192]{2,3,1,0:T(8,128)(2,1)}, u32[]{:S(2)}, u32[]{:S(2)}) async-start(bf16[4,1,256,192]{2,3,1,0:T(8,128)(2,1)} %bitcast.246), calls=%async_computation.14 | async-start | bytes 786432 | tf_op jit(solution)/shard_map/all_to_all | solution.py:64
  449.3 24.2 %all-to-all-start.13 = ((bf16[8,4,24,896]{3,2,1,0:T(8,128)(2,1)}), bf16[8,4,24,896]{3,2,1,0:T(8,128)(2,1)}, u32[]{:S(2)}, u32[]{:S(2)}) async-start(bf16[8,4,24,896]{3,2,1,0:T(8,128)(2,1)} %copy.136), calls=%async_computation.15 | async-start | bytes 2752512 | tf_op jit(solution)/shard_map/all_to_all | solution.py:64
  454.5 80.5 %reduce-scatter.8.cloned.1.call-start = ((), (), s32[]{:S(2)}) async-start(), calls=%async_computation.23 | async-start | bytes 1966080 | tf_op jit(solution)/shard_map/reduce_scatter | solution.py:313
  483.4 8.7 %copy-start.11 = (f32[8,1,770]{2,0,1:T(8,128)S(1)}, f32[8,1,770]{2,0,1:T(8,128)}, u32[]{:S(2)}) copy-start(f32[8,1,770]{2,0,1:T(8,128)} %copy.164) | copy-start | bytes 73924
  485.7 27.7 %copy-start.21 = (f32[256]{0:T(256)S(1)}, f32[256]{0:T(256)}, u32[]{:S(2)}) copy-start(f32[256]{0:T(256)} %get-tuple-element.176) | copy-start | bytes 3076
  487.9 18.9 %all-to-all-start.16 = ((bf16[8,4,24,576]{3,2,1,0:T(8,128)(2,1)}), bf16[8,4,24,576]{3,2,1,0:T(8,128)(2,1)}, u32[]{:S(2)}, u32[]{:S(2)}) async-start(bf16[8,4,24,576]{3,2,1,0:T(8,128)(2,1)} %copy.140), calls=%async_computation.19 | async-start | bytes 1966080 | tf_op jit(solution)/shard_map/all_to_all | solution.py:64
  509.0 20.8 %all-to-all-start.17 = ((bf16[4,24,1472]{2,1,0:T(8,128)(2,1)}), bf16[4,24,1472]{2,1,0:T(8,128)(2,1)}, u32[]{:S(2)}, u32[]{:S(2)}) async-start(bf16[4,24,1472]{2,1,0:T(8,128)(2,1)} %pad_maximum_fusion.1), calls=%async_computation.20 | async-start | bytes 589824 | tf_op jit(solution)/shard_map/all_to_all | solution.py:64
  513.1 58.1 %all-gather.14.cloned.1.call-start = ((), (), s32[]{:S(2)}) async-start(), calls=%async_computation.24 | async-start | bytes 1382400 | tf_op jit(solution)/shard_map/all_gather | solution.py:426
  513.4 5.9 %copy-start.16 = (f32[768]{0:T(1024)S(1)}, f32[768]{0:T(1024)}, u32[]{:S(2)}) copy-start(f32[768]{0:T(1024)} %get-tuple-element.154) | copy-start | bytes 9220
  513.4 5.9 %copy-start.17 = (f32[768]{0:T(1024)S(1)}, f32[768]{0:T(1024)}, u32[]{:S(2)}) copy-start(f32[768]{0:T(1024)} %get-tuple-element.168) | copy-start | bytes 9220
  516.3 16.6 %copy-start.13 = (f32[768]{0:T(1024)S(1)}, f32[768]{0:T(1024)}, u32[]{:S(2)}) copy-start(f32[768]{0:T(1024)} %copy-done.12) | copy-start | bytes 9220
  519.2 16.9 %copy-start.15 = (f32[256]{0:T(256)S(1)}, f32[256]{0:T(256)}, u32[]{:S(2)}) copy-start(f32[256]{0:T(256)} %copy-done.14) | copy-start | bytes 3076
  538.3 9.0 %all-to-all-start.14 = ((f32[4,1,4608]{2,1,0:T(1,128)}), f32[4,1,4608]{2,1,0:T(1,128)S(1)}, u32[]{:S(2)}, u32[]{:S(2)}) async-start(f32[4,1,4608]{2,1,0:T(1,128)} %broadcast_in_dim.145), calls=%async_computation.17 | async-start | bytes 147456 | tf_op jit(solution)/shard_map/all_to_all | solution.py:64
  559.1 9.2 %all-to-all-start.15 = ((f32[4,8,192]{2,1,0:T(8,128)}), f32[4,8,192]{2,1,0:T(8,128)S(1)}, u32[]{:S(2)}, u32[]{:S(2)}) async-start(f32[4,8,192]{2,1,0:T(8,128)} %broadcast_in_dim.146), calls=%async_computation.18 | async-start | bytes 65536 | tf_op jit(solution)/shard_map/all_to_all | solution.py:64
  (15 other events, 58.5 us)
Sparse Core Ops, SparseCore 0:
  9.6 42.9 all-gather.19
  94.8 47.2 all-gather.21
  165.6 36.1 all-gather.23
  364.0 32.5 reduce-scatter.3
  398.9 24.4 all-gather.17
  425.7 23.8 all-gather.15
  452.5 35.4 reduce-scatter.5
  490.8 39.0 reduce-scatter.7
  533.0 23.4 all-gather.13
